TPU v7x, 32 devices: a whole 2x2x4 slice. The times are simulated.
32 devices in a mesh: axial: 8 (over y, x, core), azim: 4 (over z).
Axes of the slice: x: 2, y: 2, z: 4, core: 2. Of those that a mesh axis runs over, the one named last changes fastest.
Arguments:
- state: float32 [5, 16, 1024, 96], P(None, 'axial', 'azim'), as said below
- start: float32 [5, 16, 1024, 96], P(None, 'axial', 'azim'), as said below
- modes: int32 [64], replicated, may hold values from 1 to 512, as said below
Outputs:
- section: float32 [5, 16, 1024, 96], P(None, 'axial', 'azim')
Inputs may be any that keep to these rules, and one draw needn't show every extreme that they name: Cycle j keeps the modes 0 to modes[j] - 1; modes[j] lies between 8 * (j + 1) and 2 * 8 * (j + 1), capped at 512, which the last cycle reaches. `state`: the density (field 0) lies between 0.85 and 1.15. `start`: the density (field 0) lies between 0.85 and 1.15.
All inputs are finite; a program needn't handle non-finite values.
Results may differ from a plain program's by a relative error of at most 0.00005.
Values sent between devices are 32-bit elements; how exact they have to be, the bound alone decides.
A program may use at most 64 MiB of HBM per device.

v0:
```python
import functools
import math

import jax
import jax.numpy as jnp
import numpy as np
from jax import lax
from jax.experimental import pallas as pl
from jax.experimental.pallas import tpu as pltpu
from jax.sharding import PartitionSpec as P

NTH = 1024
NIN = 64
MSTEP = 8
STEP_DT = 0.05
LANES = 128
RIM = 8
F32 = jnp.float32
BF16 = jnp.bfloat16
MESH = pl.DeviceIdType.MESH


def split_np(values):
    high = values.astype(np.float32).astype(jnp.bfloat16)
    low = (values - high.astype(np.float64)).astype(np.float32).astype(jnp.bfloat16)
    return np.stack([high, low])


@functools.lru_cache(None)
def plan(cells):
    order = np.arange(1, NIN + 1)
    kept = np.minimum(2 * MSTEP * order, NTH // 2)
    dropped = NTH // 2 + 1 - np.minimum(MSTEP * order, NTH // 2)
    use_kept = kept <= dropped
    bound = np.where(use_kept, kept, dropped)
    first_dropped = int(np.argmin(use_kept))
    ranked = np.argsort(-bound, kind="stable")
    pairs = NIN // 2
    top, bottom = ranked[:pairs], ranked[::-1][:pairs]
    rows = int(-(-np.max(bound[top] + bound[bottom]) // 32) * 32)
    wave = np.arange(rows)
    angle = lambda n, q: 2 * np.pi * ((n * q) % NTH) / NTH
    forward = []
    for waves in (wave, wave[::-1]):
        phase = angle(np.arange(cells)[None, :], waves[:, None])
        forward.append(split_np(np.concatenate([np.cos(phase), np.sin(phase)], 0)))
    inverse = []
    for waves in (wave, wave[::-1]):
        phase = angle(np.arange(-RIM, cells + RIM)[:, None], waves[None, :])
        inverse.append(split_np(np.concatenate([np.cos(phase), np.sin(phase)], 1)))
    slots = LANES // pairs
    place = np.zeros((slots + slots // 2, LANES, 2 * LANES), np.float32)
    ghost = np.zeros((slots + slots // 2, LANES, LANES), np.float32)
    for slot in range(slots):
        for pair in range(pairs):
            place[slot, top[pair], slot * pairs + pair] = 1
            place[slot, bottom[pair], LANES + slot * pairs + pair] = 1
            if bottom[pair] < 2:
                ghost[slot, slot * pairs + pair, LANES - 1 - bottom[pair]] = 1
    half = slots // 2
    for k in range(half):
        place[slots + k] = place[k] + place[half + k]
        ghost[slots + k] = ghost[k] + ghost[half + k]
    far_rows = int(-(-np.max(bound[:2]) // 16) * 16)
    far_phase = angle(
        np.arange(-RIM, cells + RIM)[:, None] + NTH // 2, np.arange(far_rows)[::-1][None, :]
    )
    far = split_np(np.concatenate([np.cos(far_phase), np.sin(far_phase)], 1))
    groups = (slots + half) // 2
    back = place.transpose(0, 2, 1)
    back = back.reshape(groups, 2, 2 * LANES, LANES).transpose(0, 2, 1, 3)
    ghost = ghost.reshape(groups, 2, LANES, LANES).transpose(0, 2, 1, 3)
    top_rows = np.tile(bound[top], slots)
    wave_of = np.where(wave[:, None] < top_rows[None, :], wave[:, None], rows - 1 - wave[:, None])
    turn = angle(cells, wave_of)
    return dict(
        rows=rows,
        far_rows=far_rows,
        far=far,
        first_dropped=first_dropped,
        top_rows=top_rows.astype(np.int32)[None],
        forward=np.stack(forward),
        inverse=np.stack(inverse),
        place=place.reshape(groups, 2 * LANES, 2 * LANES).astype(jnp.bfloat16),
        back=back.reshape(groups, 2 * LANES, 2 * LANES).astype(jnp.bfloat16),
        ghost=ghost.reshape(groups, LANES, 2 * LANES).astype(jnp.bfloat16),
        turn=np.stack([np.cos(turn), np.sin(turn)]).astype(np.float32),
    )


def split(values):
    high = values.astype(BF16)
    return high, (values - high.astype(F32)).astype(BF16)


def mm(a, b):
    return jnp.dot(a, b, preferred_element_type=F32)


def fluxes(values, direction):
    inverse = 1.0 / values[0]
    velocity = values[direction] * inverse
    kinetic = (values[1] * values[1] + values[2] * values[2] + values[3] * values[3]) * inverse
    pressure = 0.4 * (values[4] - 0.5 * kinetic)
    parts = [
        values[direction],
        values[1] * velocity,
        values[2] * velocity,
        values[3] * velocity,
        (values[4] + pressure) * velocity,
    ]
    parts[direction] = parts[direction] + pressure
    return parts, inverse, pressure


def kernel(
    cfg,
    state, modes, bounds, *refs,
):
    stored, out, refs = refs[:7], refs[7], refs[8:]
    loaded, table_sem, refs = refs[:7], refs[7], refs[8:]
    forward, inverse, place, back, ghost, turn, far_table = loaded
    (
        ext, rate, outer_own, outer_left, outer_right, inner_own, inner_left, inner_right,
        own, to_right, to_left, from_left, from_right, spectrum,
        halo_send, halo_recv, outer_send, outer_recv, inner_send, inner_recv, wave_send, wave_recv,
    ) = refs
    tables = [
        pltpu.make_async_copy(stored[k], loaded[k], table_sem.at[k]) for k in range(len(stored))
    ]
    for k in (2, 0, 5, 1, 3, 4, 6):
        tables[k].start()
    rows, first_dropped = cfg["rows"], cfg["first_dropped"]
    half, quarter = rows // 2, rows // 4
    far_rows = cfg["far_rows"]
    fields, cycles, cells = state.shape[0], state.shape[2], state.shape[3]
    tall = cells + 2 * RIM
    d, count = lax.axis_index("azim"), lax.axis_size("azim")
    a, ring = lax.axis_index("axial"), lax.axis_size("axial")
    z_right = {"azim": lax.rem(d + 1, count)}
    z_left = {"azim": lax.rem(d + count - 1, count)}
    x_right = {"axial": lax.rem(a + 1, ring)}
    x_left = {"axial": lax.rem(a + ring - 1, ring)}

    def remote(src, dst, send, recv, device):
        return pltpu.make_async_remote_copy(
            src_ref=src, dst_ref=dst, send_sem=send, recv_sem=recv,
            device_id=device, device_id_type=MESH,
        )

    barrier = pltpu.get_barrier_semaphore()
    for device in (z_right, z_left, x_right, x_left):
        pl.semaphore_signal(barrier, inc=1, device_id=device, device_id_type=MESH)
    for f in range(fields):
        for x in range(2):
            value = state[f, x]
            tail = jnp.broadcast_to(value[cycles - 1 :], (LANES - cycles, cells))
            ext[f, x, pl.ds(RIM, cells), :] = jnp.concatenate([value, tail], axis=0).T
    for f in range(fields):
        low_lane = lax.broadcasted_iota(jnp.int32, (cells, LANES), 1) < LANES // 2
        outer_own[f] = jnp.where(
            low_lane,
            pltpu.roll(ext[f, 1, pl.ds(RIM, cells), :], LANES // 2, 1),
            ext[f, 0, pl.ds(RIM, cells), :],
        )
    pl.semaphore_wait(barrier, 4)

    halos = [
        remote(
            ext.at[:, :, pl.ds(cells, RIM)], ext.at[:, :, pl.ds(0, RIM)],
            halo_send.at[0], halo_recv.at[0], z_right,
        ),
        remote(
            ext.at[:, :, pl.ds(RIM, RIM)], ext.at[:, :, pl.ds(cells + RIM, RIM)],
            halo_send.at[1], halo_recv.at[1], z_left,
        ),
    ]
    outers = [
        remote(outer_own, outer_left, outer_send.at[0], outer_recv.at[0], x_right),
        remote(outer_own, outer_right, outer_send.at[1], outer_recv.at[1], x_left),
    ]
    chunks = 10
    rights = [
        remote(to_right.at[c], from_left.at[c], wave_send.at[0, c], wave_recv.at[0, c], z_right)
        for c in range(chunks)
    ]
    lefts = [
        remote(to_left.at[c], from_right.at[c], wave_send.at[1, c], wave_recv.at[1, c], z_left)
        for c in range(chunks)
    ]
    inners = [
        [
            remote(inner_own.at[f], inner_left.at[f], inner_send.at[0, f], inner_recv.at[0, f], x_right),
            remote(inner_own.at[f], inner_right.at[f], inner_send.at[1, f], inner_recv.at[1, f], x_left),
        ]
        for f in range(fields)
    ]
    is_first, is_last = d == 0, d == count - 1

    lane_cells = lax.broadcasted_iota(jnp.int32, (cells, LANES), 1)
    parity_cells = (1 - 2 * (lax.broadcasted_iota(jnp.int32, (cells, LANES), 0) & 1)).astype(F32)
    signs = jnp.where(lane_cells >= first_dropped, parity_cells, 1.0)
    row_ids = lax.broadcasted_iota(jnp.int32, (quarter, LANES), 0)
    low_lanes = lax.broadcasted_iota(jnp.int32, (quarter, LANES), 1) < LANES // 2
    tables[2].wait()
    top_rows = bounds[...]
    cycle_ids = lax.broadcasted_iota(jnp.int32, (8, NIN), 1)
    kept_modes = jnp.broadcast_to(modes[...], (8, NIN))
    counts = split(
        jnp.where(cycle_ids < first_dropped, kept_modes, NTH // 2 + 1 - kept_modes).astype(F32)
    )
    last = place.shape[0] - 1
    keep = sum(
        mm(term, place[last, pl.ds(first, NIN), :]) for term in counts for first in (0, LANES)
    )
    top_keep, bottom_keep = keep[0:1, :LANES], keep[0:1, LANES:]

    def tile_fields(tile):
        if tile < 2:
            return [(2 * tile, 0), (2 * tile + 1, 1)]
        return [(4, 2)]

    def tile_chunks(tile):
        return range(4 * tile, 4 * tile + 4) if tile < 2 else range(8, 10)

    for copy in halos + outers:
        copy.start()
    tables[0].wait()
    for tile in range(3):
        high = jnp.zeros((cells, 2 * LANES), F32)
        low = jnp.zeros((cells, 2 * LANES), F32)
        for f, group in tile_fields(tile):
            planes = [ext[f, x, pl.ds(RIM, cells), :] * signs for x in range(2)]
            field_high, field_low = split(jnp.concatenate(planes, axis=1))
            high = high + mm(field_high, place[group])
            low = low + mm(field_low, place[group])
        high, low = high.astype(BF16), low.astype(BF16)
        for part in range(2):
            window = pl.ds(part * rows, rows)
            sums = []
            for which in range(2):
                lanes = slice(which * LANES, (which + 1) * LANES)
                both = mm(
                    forward[which, 0, window, :],
                    jnp.concatenate([high[:, lanes], low[:, lanes]], axis=1),
                )
                sums.append(
                    both[:, :LANES]
                    + both[:, LANES:]
                    + mm(forward[which, 1, window, :], high[:, lanes])
                )
            pieces = []
            for side in range(4):
                part_rows = slice(side * quarter, (side + 1) * quarter)
                pieces.append(
                    jnp.where(
                        row_ids + side * quarter < top_rows, sums[0][part_rows], sums[1][part_rows]
                    )
                )
            for k, c in enumerate(tile_chunks(tile)):
                own[c, part] = pieces[k] if tile < 2 else jnp.where(low_lanes, pieces[k], pieces[k + 2])
        for c in tile_chunks(tile):
            @pl.when(is_first)
            def _():
                to_right[c] = own[c]
                rights[c].start()

            @pl.when(is_last)
            def _():
                to_left[c] = own[c]
                lefts[c].start()

    for copy in halos:
        copy.wait()
    for k in (5, 1, 3, 4, 6):
        tables[k].wait()

    def turned(ref, c, sign):
        if c < 8:
            window = pl.ds((c % 4) * quarter, quarter)
            u, v = turn[0, window, :], turn[1, window, :]
        else:
            low_window = pl.ds((c - 8) * quarter, quarter)
            high_window = pl.ds(half + (c - 8) * quarter, quarter)
            u = jnp.where(low_lanes, turn[0, low_window, :], turn[0, high_window, :])
            v = jnp.where(low_lanes, turn[1, low_window, :], turn[1, high_window, :])
        v = v * sign
        cosine, sine = ref[c, 0], ref[c, 1]
        return u * cosine + v * sine, u * sine - v * cosine

    inside = jnp.logical_not(is_first) & jnp.logical_not(is_last)
    near_first = 2 * d < count

    def pass_right(c, when):
        @pl.when(when & jnp.logical_not(is_first))
        def _():
            rights[c].wait_recv()

        @pl.when(when & inside)
        def _():
            cosine, sine = turned(from_left, c, 1.0)
            to_right[c, 0] = own[c, 0] + cosine
            to_right[c, 1] = own[c, 1] + sine
            rights[c].start()

    def pass_left(c, when):
        @pl.when(when & jnp.logical_not(is_last))
        def _():
            lefts[c].wait_recv()

        @pl.when(when & inside)
        def _():
            cosine, sine = turned(from_right, c, -1.0)
            to_left[c, 0] = own[c, 0] + cosine
            to_left[c, 1] = own[c, 1] + sine
            lefts[c].start()

    def relay_near(c):
        pass_right(c, near_first)
        pass_left(c, jnp.logical_not(near_first))

    def relay_far(c):
        pass_left(c, near_first)
        pass_right(c, jnp.logical_not(near_first))

        @pl.when(jnp.logical_not(is_first))
        def _():
            cosine, sine = turned(from_left, c, 1.0)
            own[c, 0] = own[c, 0] + cosine
            own[c, 1] = own[c, 1] + sine

        @pl.when(jnp.logical_not(is_last))
        def _():
            cosine, sine = turned(from_right, c, -1.0)
            own[c, 0] = own[c, 0] + cosine
            own[c, 1] = own[c, 1] + sine

    lane_tall = lax.broadcasted_iota(jnp.int32, (tall, LANES), 1)
    parity_tall = (1 - 2 * (lax.broadcasted_iota(jnp.int32, (tall, LANES), 0) & 1)).astype(F32)

    def restore(tile):
        for side in range(4):
            row = row_ids + side * quarter
            back_row = rows - 1 - row
            top_weight = jnp.where(
                row.astype(F32) < top_keep, jnp.where(row == 0, 1.0 / NTH, 2.0 / NTH), 0.0
            )
            bottom_weight = jnp.where(
                back_row.astype(F32) < bottom_keep,
                jnp.where(back_row == 0, 1.0 / NTH, 2.0 / NTH),
                0.0,
            )
            if tile == 2:
                mine = low_lanes if side < 2 else jnp.logical_not(low_lanes)
                top_weight = jnp.where(mine, top_weight, 0.0)
                bottom_weight = jnp.where(mine, bottom_weight, 0.0)
            c = 4 * tile + side if tile < 2 else 8 + side % 2
            for part in range(2):
                waves = own[c, part]
                window = pl.ds(part * rows + side * quarter, quarter)
                for which, weight in ((0, top_weight), (1, bottom_weight)):
                    weighted = split(waves * weight)
                    spectrum[which, window, pl.ds(0, LANES)] = weighted[0]
                    spectrum[which, window, pl.ds(LANES, LANES)] = weighted[1]

        def series(which):
            both = mm(inverse[which, 0], spectrum[which])
            return (
                both[:, :LANES]
                + both[:, LANES:]
                + mm(inverse[which, 1], spectrum[which, :, pl.ds(0, LANES)])
            )

        near = split(jnp.concatenate([series(0), series(1)], axis=1))
        waves = jnp.concatenate(
            [spectrum[1, pl.ds((part + 1) * rows - far_rows, far_rows), :] for part in range(2)],
            axis=0,
        )
        both = mm(far_table[0], waves)
        far = split(both[:, :LANES] + both[:, LANES:] + mm(far_table[1], waves[:, :LANES]))
        for f, group in tile_fields(tile):
            filtered = mm(near[0], back[group]) + mm(near[1], back[group])
            across = mm(far[0], ghost[group]) + mm(far[1], ghost[group])
            across = -across if f in (2, 3) else across
            for x in range(2):
                lanes = slice(x * LANES, (x + 1) * LANES)
                raw = ext[f, x]
                now = jnp.where(
                    lane_tall >= first_dropped,
                    raw - parity_tall * filtered[:, lanes],
                    filtered[:, lanes],
                )
                ext[f, x] = jnp.where(lane_tall >= LANES - 2, across[:, lanes], now)
            centre = pl.ds(RIM, cells)
            inner_own[f] = jnp.where(
                lane_cells < LANES // 2,
                ext[f, 0, centre, :],
                pltpu.roll(ext[f, 1, centre, :], LANES // 2, 1),
            )
            for copy in inners[f]:
                copy.start()

    lag = 3
    for step in range(chunks + lag):
        if step < chunks:
            relay_near(step)
        c = step - lag
        if c >= 0:
            relay_far(c)
            if c in (3, 7, 9):
                restore(c // 4)

    block = min(32, cells)
    deep = block + 2 * RIM
    lane_deep = lax.broadcasted_iota(jnp.int32, (deep, LANES), 1)
    lane_block = lax.broadcasted_iota(jnp.int32, (block, LANES), 1)
    radius = jnp.where(lane_block >= LANES - 2, lane_block - LANES, lane_block).astype(F32) + 0.5
    inv_radius = 1.0 / radius
    angular = inv_radius * (1.0 / (12.0 * (2.0 * math.pi / NTH)))
    radial = inv_radius * (1.0 / 12.0)

    @pl.loop(0, 2 * (cells // block))
    def _(step):
        x = step % 2
        start = pl.multiple_of((step // 2) * block, block)
        values = [ext[f, x, pl.ds(start, deep), :] for f in range(fields)]
        around, _, _ = fluxes(values, 3)
        centre = [value[RIM : RIM + block] for value in values]
        outward, inverse_density, pressure = fluxes(centre, 2)
        sources = [
            None,
            None,
            (centre[3] * centre[3] * inverse_density + pressure) * inv_radius,
            -(centre[2] * centre[3] * inverse_density) * inv_radius,
            None,
        ]
        for f in range(fields):
            g = around[f]
            turn_term = (
                8.0 * (pltpu.roll(g, deep - 1, 0) - pltpu.roll(g, 1, 0))
                - (pltpu.roll(g, deep - 2, 0) - pltpu.roll(g, 2, 0))
            )[RIM : RIM + block]
            g = outward[f] * radius
            out_term = 8.0 * (pltpu.roll(g, LANES - 1, 1) - pltpu.roll(g, 1, 1)) - (
                pltpu.roll(g, LANES - 2, 1) - pltpu.roll(g, 2, 1)
            )
            total = -(turn_term * angular + out_term * radial)
            if sources[f] is not None:
                total = total + sources[f]
            rate[f, x, pl.ds(start, block), :] = STEP_DT * total

    for copy in outers:
        copy.wait_recv()
    for pair in inners:
        for copy in pair:
            copy.wait_recv()

    low_block = lane_block < LANES // 2

    @pl.loop(0, cells // block)
    def _(step):
        window = pl.ds(pl.multiple_of(step * block, block), block)

        def axial_term(mid, left, right, swapped):
            mids = fluxes([mid[f, window, :] for f in range(fields)], 1)[0]
            lefts_ = fluxes([left[f, window, :] for f in range(fields)], 1)[0]
            rights_ = fluxes([right[f, window, :] for f in range(fields)], 1)[0]
            terms = []
            for f in range(fields):
                back_step, fore_step = mids[f] - lefts_[f], rights_[f] - mids[f]
                if swapped:
                    mixed = jnp.where(low_block, back_step, fore_step)
                else:
                    mixed = jnp.where(low_block, fore_step, back_step)
                terms.append(8.0 * pltpu.roll(mixed, LANES // 2, 1) - (rights_[f] - lefts_[f]))
            return terms

        inner = axial_term(inner_own, inner_left, inner_right, False)
        outer = axial_term(outer_own, outer_left, outer_right, True)
        for f in range(fields):
            first = jnp.where(low_block, inner[f], outer[f])
            second = pltpu.roll(jnp.where(low_block, outer[f], inner[f]), LANES // 2, 1)
            for x, term in ((0, first), (1, second)):
                rate[f, x, window, :] = rate[f, x, window, :] - (STEP_DT / 12.0) * term

    for f in range(fields):
        for x in range(2):
            out[f, x] = rate[f, x].T[:cycles]

    for copy in outers:
        copy.wait_send()
    for pair in inners:
        for copy in pair:
            copy.wait_send()
    for c in range(chunks):
        @pl.when(jnp.logical_not(is_last))
        def _():
            rights[c].wait_send()

        @pl.when(jnp.logical_not(is_first))
        def _():
            lefts[c].wait_send()


def shards(state, start, modes):
    fields, axial, cells, cycles = state.shape
    cfg = plan(cells)
    rows = cfg["rows"]
    turned = state.transpose(0, 1, 3, 2)
    plane = (fields, cells, LANES)
    chunk = (10, 2, rows // 4, LANES)
    names = ("forward", "inverse", "place", "back", "ghost", "turn", "far")
    tables = [jnp.asarray(cfg[name]) for name in names]
    vmem = pl.BlockSpec(memory_space=pltpu.VMEM)
    step = pl.pallas_call(
        functools.partial(kernel, cfg),
        out_shape=jax.ShapeDtypeStruct(turned.shape, F32),
        in_specs=[vmem] * 3 + [pl.BlockSpec(memory_space=pltpu.HBM)] * 7,
        out_specs=vmem,
        scratch_shapes=[pltpu.VMEM(table.shape, table.dtype) for table in tables]
        + [pltpu.SemaphoreType.DMA((7,))]
        + [pltpu.VMEM((fields, axial, cells + 2 * RIM, LANES), F32)]
        + [pltpu.VMEM((fields, axial, cells, LANES), F32)]
        + [pltpu.VMEM(plane, F32)] * 6
        + [pltpu.VMEM(chunk, F32)] * 5
        + [pltpu.VMEM((2, 2 * rows, 2 * LANES), BF16)]
        + [
            pltpu.SemaphoreType.DMA((2,)),
            pltpu.SemaphoreType.DMA((2,)),
            pltpu.SemaphoreType.DMA((2,)),
            pltpu.SemaphoreType.DMA((2,)),
            pltpu.SemaphoreType.DMA((2, fields)),
            pltpu.SemaphoreType.DMA((2, fields)),
            pltpu.SemaphoreType.DMA((2, 10)),
            pltpu.SemaphoreType.DMA((2, 10)),
        ],
        compiler_params=pltpu.CompilerParams(
            collective_id=0, has_side_effects=True, vmem_limit_bytes=48 * 1024 * 1024
        ),
        name="jet_section",
    )(
        turned,
        modes.reshape(1, NIN),
        jnp.asarray(cfg["top_rows"]),
        *tables,
    )
    return start + step.transpose(0, 1, 3, 2)


def solution(mesh):
    in_specs = (P(None, "axial", "azim", None), P(None, "axial", "azim", None), P())
    out_specs = P(None, "axial", "azim", None)
    return jax.shard_map(shards, mesh=mesh, in_specs=in_specs, out_specs=out_specs, check_vma=False)
```

profile of v0, /device:TPU:1, one launch (start us, length us, event | category | flops | bytes accessed | tf_op | source)
XLA Modules:
  0.0 58.1 jit_solution(15364684678606127987)
XLA Ops:
  0.0 0.0 copy-start
  0.0 1.4 %copy-done = bf16[2,2,704,256]{3,2,1,0:T(8,128)(2,1)S(1)} copy-done((bf16[2,2,704,256]{3,2,1,0:T(8,128)(2,1)S(1)}, bf16[2,2,704,256]{3,2,1,0:T(8,128)(2,1)}, u32[]{:S(2)}) %copy-start) | copy-done | bytes 1441816
  1.4 0.0 copy-start.1
  1.4 1.2 %copy-done.1 = f32[5,2,256,96]{2,3,1,0:T(8,128)S(1)} copy-done((f32[5,2,256,96]{2,3,1,0:T(8,128)S(1)}, f32[5,2,256,96]{2,3,1,0:T(8,128)}, u32[]{:S(2)}) %copy-start.1) | copy-done | bytes 983064
  2.6 0.0 copy-start.2
  2.6 1.0 %copy-done.2 = bf16[3,256,256]{2,1,0:T(8,128)(2,1)S(1)} copy-done((bf16[3,256,256]{2,1,0:T(8,128)(2,1)S(1)}, bf16[3,256,256]{2,1,0:T(8,128)(2,1)}, u32[]{:S(2)}) %copy-start.2) | copy-done | bytes 393240
  3.6 0.0 copy-start.3
  3.6 1.0 %copy-done.3 = bf16[3,256,256]{2,1,0:T(8,128)(2,1)S(1)} copy-done((bf16[3,256,256]{2,1,0:T(8,128)(2,1)S(1)}, bf16[3,256,256]{2,1,0:T(8,128)(2,1)}, u32[]{:S(2)}) %copy-start.3) | copy-done | bytes 393240
  4.6 0.0 copy-start.4
  4.6 1.0 %copy-done.4 = f32[2,352,128]{2,1,0:T(8,128)S(1)} copy-done((f32[2,352,128]{2,1,0:T(8,128)S(1)}, f32[2,352,128]{2,1,0:T(8,128)}, u32[]{:S(2)}) %copy-start.4) | copy-done | bytes 360472
  5.5 0.0 copy-start.5
  5.5 0.9 %copy-done.5 = bf16[3,128,256]{2,1,0:T(8,128)(2,1)S(1)} copy-done((bf16[3,128,256]{2,1,0:T(8,128)(2,1)S(1)}, bf16[3,128,256]{2,1,0:T(8,128)(2,1)}, u32[]{:S(2)}) %copy-start.5) | copy-done | bytes 196632
  6.5 0.0 copy-start.6
  6.5 0.9 %copy-done.6 = bf16[2,272,64]{2,1,0:T(8,128)(2,1)S(1)} copy-done((bf16[2,272,64]{2,1,0:T(8,128)(2,1)S(1)}, bf16[2,272,64]{2,1,0:T(8,128)(2,1)}, u32[]{:S(2)}) %copy-start.6) | copy-done | bytes 69656
  7.4 0.0 copy-start.7
  7.4 0.7 %copy-done.7 = s32[64]{0:T(128)S(1)} copy-done((s32[64]{0:T(128)S(1)}, s32[64]{0:T(128)}, u32[]{:S(2)}) %copy-start.7) | copy-done | bytes 280
  8.0 0.0 copy-start.8
  8.0 0.7 %copy-done.8 = s32[1,128]{1,0:T(1,128)S(1)} copy-done((s32[1,128]{1,0:T(1,128)S(1)}, s32[1,128]{1,0:T(1,128)}, u32[]{:S(2)}) %copy-start.8) | copy-done | bytes 536
  8.7 0.0 copy-start.9
  8.7 48.3 %jet_section.1 = f32[5,2,96,256]{3,2,1,0:T(8,128)S(1)} custom-call(f32[5,2,96,256]{3,2,1,0:T(8,128)S(1)} %bitcast.4, s32[1,64]{1,0:T(1,128)S(1)} %bitcast.5, s32[1,128]{1,0:T(1,128)S(1)} %copy-done.8, bf16[2,2,704,256]{3,2,1,0:T(8,128)(2,1)S(1)} %copy-done, bf16[2,2,272,704]{3,2,1,0:T(8,128)(2,1)} %constant.17.clone.refs_1_, ...), custom_call_target="tpu_custom_call" | custom-call | tf_op jit(solution)/shard_map/jet_section/pallas_call | solution.py:515
  57.0 0.0 copy-done.9
  57.0 1.1 %bitcast_add_fusion = f32[5,2,256,96]{2,3,1,0:T(8,128)} fusion(f32[5,2,256,96]{2,3,1,0:T(8,128)S(1)} %copy-done.9, f32[5,2,96,256]{3,2,1,0:T(8,128)S(1)} %jet_section.1), kind=kLoop, calls=%fused_computation | loop fusion | flops 245760 | bytes 2949120 | tf_op jit(solution)/shard_map/add | solution.py:547
Async XLA Ops:
  0.0 1.4 %copy-start = (bf16[2,2,704,256]{3,2,1,0:T(8,128)(2,1)S(1)}, bf16[2,2,704,256]{3,2,1,0:T(8,128)(2,1)}, u32[]{:S(2)}) copy-start(bf16[2,2,704,256]{3,2,1,0:T(8,128)(2,1)} %constant.16.clone.refs_0_) | copy-start | bytes 4325380
  1.4 1.2 %copy-start.1 = (f32[5,2,256,96]{2,3,1,0:T(8,128)S(1)}, f32[5,2,256,96]{2,3,1,0:T(8,128)}, u32[]{:S(2)}) copy-start(f32[5,2,256,96]{2,3,1,0:T(8,128)} %param.11) | copy-start | bytes 2949124
  2.6 1.0 %copy-start.2 = (bf16[3,256,256]{2,1,0:T(8,128)(2,1)S(1)}, bf16[3,256,256]{2,1,0:T(8,128)(2,1)}, u32[]{:S(2)}) copy-start(bf16[3,256,256]{2,1,0:T(8,128)(2,1)} %constant.19.clone.refs_3_) | copy-start | bytes 1179652
  3.6 1.0 %copy-start.3 = (bf16[3,256,256]{2,1,0:T(8,128)(2,1)S(1)}, bf16[3,256,256]{2,1,0:T(8,128)(2,1)}, u32[]{:S(2)}) copy-start(bf16[3,256,256]{2,1,0:T(8,128)(2,1)} %constant.18.clone.refs_2_) | copy-start | bytes 1179652
  4.6 1.0 %copy-start.4 = (f32[2,352,128]{2,1,0:T(8,128)S(1)}, f32[2,352,128]{2,1,0:T(8,128)}, u32[]{:S(2)}) copy-start(f32[2,352,128]{2,1,0:T(8,128)} %constant.21.clone.refs_5_) | copy-start | bytes 1081348
  5.5 0.9 %copy-start.5 = (bf16[3,128,256]{2,1,0:T(8,128)(2,1)S(1)}, bf16[3,128,256]{2,1,0:T(8,128)(2,1)}, u32[]{:S(2)}) copy-start(bf16[3,128,256]{2,1,0:T(8,128)(2,1)} %constant.20.clone.refs_4_) | copy-start | bytes 589828
  6.5 0.9 %copy-start.6 = (bf16[2,272,64]{2,1,0:T(8,128)(2,1)S(1)}, bf16[2,272,64]{2,1,0:T(8,128)(2,1)}, u32[]{:S(2)}) copy-start(bf16[2,272,64]{2,1,0:T(8,128)(2,1)} %constant.22.clone.refs_6_) | copy-start | bytes 208900
  7.4 0.7 %copy-start.7 = (s32[64]{0:T(128)S(1)}, s32[64]{0:T(128)}, u32[]{:S(2)}) copy-start(s32[64]{0:T(128)} %param.13) | copy-start | bytes 772
  8.0 0.7 %copy-start.8 = (s32[1,128]{1,0:T(1,128)S(1)}, s32[1,128]{1,0:T(1,128)}, u32[]{:S(2)}) copy-start(s32[1,128]{1,0:T(1,128)} %constant.23.clone.bounds) | copy-start | bytes 1540
  8.7 48.3 %copy-start.9 = (f32[5,2,256,96]{2,3,1,0:T(8,128)S(1)}, f32[5,2,256,96]{2,3,1,0:T(8,128)}, u32[]{:S(2)}) copy-start(f32[5,2,256,96]{2,3,1,0:T(8,128)} %param.12) | copy-start | bytes 2949124
where the time goes:
time: 58.4 us; the launch traced here: 58.1 us
  Pallas kernels  48.3 us (83%)
  local copies, waits for them, and re-layouts  8.68 us (15%)
  other arithmetic  1.12 us (2%)
    pallas_call x1, Pallas kernels, shards(): pl.pallas_call(functools.partial(kernel, cfg), out_shape=jax.ShapeDtypeSt...  48.3 us
    unnamed x20, local copies, waits for them, and re-layouts  8.68 us

commit v1 on v0

v1 whole, which is shorter than its diff:
```python
import functools
import math

import jax
import jax.numpy as jnp
import numpy as np
from jax import lax
from jax.experimental import pallas as pl
from jax.experimental.pallas import tpu as pltpu
from jax.sharding import PartitionSpec as P

STEP_DT = 0.05
LANES = 128
CHUNKS = 2
BLOCK = 16
FLOOR = 1e-9
F32 = jnp.float32
BF16 = jnp.bfloat16
MESH = pl.DeviceIdType.MESH


def split_np(values):
    high = values.astype(np.float32).astype(jnp.bfloat16)
    low = (values - high.astype(np.float64)).astype(np.float32).astype(jnp.bfloat16)
    return high, low


def round_up(value, multiple):
    return -(-value // multiple) * multiple


@functools.lru_cache(None)
def plan(cells, count):
    total = cells * count
    width = round_up(cells, LANES)
    where = np.arange(cells)

    def coupling(offset):
        distance = offset * cells + where[:, None] - where[None, :]
        sine = np.sin(np.pi * distance / total)
        return np.where(distance == 0, 0.0, 1.0 / (total * np.where(distance == 0, 1.0, sine)))

    def wide(rows):
        return np.concatenate([rows] * (width // cells), axis=1)

    def padded(rows):
        return np.pad(rows, ((0, 0), (0, width - cells)))

    local = np.zeros((width, width))
    local[:cells] = wide(coupling(0).T)
    starts, ranks, outgoing, incoming = [], [], [], []
    for offset in range(1, count):
        left, values, right = np.linalg.svd(coupling(offset))
        rank = round_up(max(int(np.sum(values > FLOOR)), 1), 8)
        starts.append(sum(ranks))
        ranks.append(rank)
        outgoing.append(padded(right[:rank]))
        incoming.append(wide((left[:, :rank] * values[:rank]).T))
    depth = sum(ranks)
    out_high, out_low = split_np(np.concatenate(outgoing))
    in_high, in_low = split_np(np.concatenate(incoming))
    stacked = round_up(3 * depth, LANES)
    blank = np.zeros((stacked - 3 * depth, width), jnp.bfloat16)
    table = np.concatenate([*split_np(local), out_high, out_low, in_high, in_high, in_low, blank])
    return dict(width=width, depth=depth, stacked=stacked, starts=starts, ranks=ranks, table=table)


def split(values):
    high = values.astype(BF16)
    return high, (values - high.astype(F32)).astype(BF16)


def mm(a, b):
    return jnp.dot(a, b, preferred_element_type=F32)


def pressure_of(values, inverse):
    kinetic = (values[1] * values[1] + values[2] * values[2] + values[3] * values[3]) * inverse
    return 0.4 * (values[4] - 0.5 * kinetic)


def fluxes(values, direction, inverse, pressure):
    velocity = values[direction] * inverse
    parts = [
        values[direction],
        values[1] * velocity,
        values[2] * velocity,
        values[3] * velocity,
        (values[4] + pressure) * velocity,
    ]
    parts[direction] = parts[direction] + pressure
    return parts


def turns(steps, total):
    quarter = total // 2
    quadrant = (steps + quarter // 2) // quarter
    angle = (steps - quadrant * quarter).astype(F32) * (math.pi / total)
    square = angle * angle
    sine = angle + angle * square * (
        -1.0 / 6 + square * (1.0 / 120 + square * (-1.0 / 5040 + square * (1.0 / 362880)))
    )
    cosine = 1.0 + square * (
        -0.5
        + square * (1.0 / 24 + square * (-1.0 / 720 + square * (1.0 / 40320 - square * (1.0 / 3628800))))
    )
    odd = (quadrant & 1) == 1
    first, second = jnp.where(odd, cosine, sine), jnp.where(odd, sine, cosine)
    return (
        jnp.where((quadrant & 2) == 2, -first, first),
        jnp.where(((quadrant + 1) & 2) == 2, -second, second),
    )


def kernel(
    cfg,
    state_hbm, modes_hbm, table_hbm, out,
    state, modes, table, cosines, sines,
    x_high, x_low, near, mom_own, mom_in,
    fx_own, fx_left, fx_right, g_turn, g_out, rate,
    edge_right, edge_left, edge_from_left, edge_from_right, ghost,
    load_sem, mom_send, mom_recv, fx_send, fx_recv, edge_send, edge_recv,
):
    fields, axial, cycles, width = state.shape
    cells, inner = cfg["cells"], modes.shape[1]
    depth, stacked = cfg["depth"], cfg["stacked"]
    starts, ranks = cfg["starts"], cfg["ranks"]
    count, ring = lax.axis_size("azim"), lax.axis_size("axial")
    d, a = lax.axis_index("azim"), lax.axis_index("axial")
    total = cells * count
    planes = [(f, x) for f in range(fields) for x in range(axial)]
    span = inner // CHUNKS

    def z_at(offset):
        return {"azim": lax.rem(d + offset, count)}

    x_right = {"axial": lax.rem(a + 1, ring)}
    x_left = {"axial": lax.rem(a + ring - 1, ring)}

    def remote(src, dst, send, recv, device):
        return pltpu.make_async_remote_copy(
            src_ref=src, dst_ref=dst, send_sem=send, recv_sem=recv,
            device_id=device, device_id_type=MESH,
        )

    outer_rows, inner_rows = pl.ds(inner, cycles - inner), pl.ds(0, inner)
    loads = [
        pltpu.make_async_copy(modes_hbm, modes, load_sem.at[0]),
        pltpu.make_async_copy(
            state_hbm.at[:, :, outer_rows], state.at[:, :, outer_rows], load_sem.at[1]
        ),
        pltpu.make_async_copy(
            state_hbm.at[:, :, inner_rows], state.at[:, :, inner_rows], load_sem.at[2]
        ),
        pltpu.make_async_copy(table_hbm, table, load_sem.at[3]),
    ]
    for copy in loads:
        copy.start()

    barrier = pltpu.get_barrier_semaphore()
    peers = [z_at(offset) for offset in range(1, count)] + [x_right, x_left]
    for device in peers:
        pl.semaphore_signal(barrier, inc=1, device_id=device, device_id_type=MESH)

    moments = [
        [
            remote(
                mom_own.at[c, pl.ds(starts[k], ranks[k])], mom_in.at[c, pl.ds(starts[k], ranks[k])],
                mom_send.at[c, k], mom_recv.at[c, k], z_at(k + 1),
            )
            for k in range(len(ranks))
        ]
        for c in range(CHUNKS)
    ]
    pieces = [pl.ds(c * span, span) for c in range(CHUNKS)] + [outer_rows]
    crossings = [
        [
            remote(
                fx_own.at[:, :, rows], fx_left.at[:, :, rows], fx_send.at[0, k], fx_recv.at[0, k], x_right
            ),
            remote(
                fx_own.at[:, :, rows], fx_right.at[:, :, rows], fx_send.at[1, k], fx_recv.at[1, k], x_left
            ),
        ]
        for k, rows in enumerate(pieces)
    ]
    edges = [
        remote(edge_right, edge_from_left, edge_send.at[0], edge_recv.at[0], z_at(1)),
        remote(edge_left, edge_from_right, edge_send.at[1], edge_recv.at[1], z_at(count - 1)),
        remote(
            g_out.at[:, :, pl.ds(0, 8)], ghost, edge_send.at[2], edge_recv.at[2], z_at(count // 2)
        ),
    ]

    loads[0].wait()
    kept = jnp.broadcast_to(modes[...], (inner, inner)).astype(F32)
    same = lax.broadcasted_iota(jnp.int32, (inner, inner), 0) == lax.broadcasted_iota(
        jnp.int32, (inner, inner), 1
    )
    odd_count = 2.0 * jnp.sum(jnp.where(same, kept, 0.0), axis=1, keepdims=True) - 1.0
    share = odd_count * (1.0 / total)
    lane = lax.broadcasted_iota(jnp.int32, (inner, width), 1)
    place = (lax.rem(lane, cells) + d * cells).astype(F32)
    steps = (odd_count * place).astype(jnp.int32) & (2 * total - 1)
    sine, cosine = turns(steps, total)
    sines[...] = sine
    cosines[...] = cosine

    def axial_flux(values, x, rows):
        inverse = 1.0 / values[0]
        for f, part in enumerate(fluxes(values, 1, inverse, pressure_of(values, inverse))):
            fx_own[f, x, rows, :] = part

    loads[1].wait()
    for first in range(inner, cycles, BLOCK):
        rows = pl.ds(first, BLOCK)
        for x in range(axial):
            axial_flux([state[f, x, rows, :] for f in range(fields)], x, rows)
    pl.semaphore_wait(barrier, len(peers))
    for copy in crossings[CHUNKS]:
        copy.start()

    loads[2].wait()
    loads[3].wait()
    out_table = table[pl.ds(2 * width, 2 * depth), :]
    contract_lanes = (((1,), (1,)), ((), ()))
    for c in range(CHUNKS):
        rows = pl.ds(c * span, span)
        for p, (f, x) in enumerate(planes):
            value = state[f, x, rows, :]
            for part, wave in enumerate((cosines, sines)):
                high, low = split(value * wave[rows, :])
                slot = pl.ds((2 * p + part) * span, span)
                x_high[c, slot, :] = high
                x_low[c, slot, :] = low
        sums = lax.dot_general(
            out_table, x_high[c], contract_lanes, preferred_element_type=F32
        ) + lax.dot_general(out_table, x_low[c], contract_lanes, preferred_element_type=F32)
        sums = sums[:depth] + sums[depth:]
        for k in range(len(ranks)):
            wrapped = (1 - 2 * ((d + k + 1) // count)).astype(F32)
            mom_own[c, pl.ds(starts[k], ranks[k]), :] = (
                sums[starts[k] : starts[k] + ranks[k]] * wrapped
            )
        for copy in moments[c]:
            copy.start()

    local_high, local_low = table[pl.ds(0, width), :], table[pl.ds(width, width), :]
    for c in range(CHUNKS):
        near[c] = mm(x_high[c], local_high) + mm(x_low[c], local_high) + mm(x_high[c], local_low)

    in_table = table[pl.ds(2 * width + 2 * depth, stacked), :]
    for c in range(CHUNKS):
        for copy in moments[c]:
            copy.wait_recv()
        high = mom_in[c].astype(BF16).astype(F32)
        low = (mom_in[c] - high).astype(BF16).astype(F32)
        parts = [high, low, high]
        if stacked > 3 * depth:
            parts.append(jnp.zeros((stacked - 3 * depth, high.shape[1]), F32))
        stack = jnp.concatenate(parts, axis=0).T.astype(BF16)
        near[c] = near[c] + mm(stack, in_table)
        for first in range(0, span, BLOCK):
            rows = pl.ds(c * span + first, BLOCK)
            wave_sine, wave_cosine = sines[rows, :], cosines[rows, :]
            weight = share[c * span + first : c * span + first + BLOCK]
            for x in range(axial):
                values = []
                for f in range(fields):
                    slot = 2 * (f * axial + x) * span + first
                    kept_value = (
                        wave_sine * near[c, pl.ds(slot, BLOCK), :]
                        - wave_cosine * near[c, pl.ds(slot + span, BLOCK), :]
                        + weight * state[f, x, rows, :]
                    )
                    state[f, x, rows, :] = kept_value
                    values.append(kept_value)
                axial_flux(values, x, rows)
        for copy in crossings[c]:
            copy.start()

    radius_of = lambda first, size: (
        lax.broadcasted_iota(jnp.int32, (size, width), 0) + first
    ).astype(F32) + 0.5
    for first in range(0, cycles, BLOCK):
        rows = pl.ds(first, BLOCK)
        radius = radius_of(first, BLOCK)
        inv_radius = 1.0 / radius
        for x in range(axial):
            values = [state[f, x, rows, :] for f in range(fields)]
            inverse = 1.0 / values[0]
            pressure = pressure_of(values, inverse)
            for f, part in enumerate(fluxes(values, 3, inverse, pressure)):
                g_turn[f, x, rows, :] = part
            for f, part in enumerate(fluxes(values, 2, inverse, pressure)):
                g_out[f, x, rows, :] = part * radius
            rate[2, x, rows, :] = (values[3] * values[3] * inverse + pressure) * inv_radius
            rate[3, x, rows, :] = -(values[2] * values[3] * inverse) * inv_radius

    edge_lane = lax.broadcasted_iota(jnp.int32, (cycles, LANES), 1)
    pack_right = jnp.zeros((cycles, LANES), F32)
    pack_left = jnp.zeros((cycles, LANES), F32)
    for p, (f, x) in enumerate(planes):
        mine = (edge_lane >> 1) == p
        ends = g_turn[f, x, :, pl.ds(width - LANES, LANES)]
        pack_right = jnp.where(mine, pltpu.roll(ends, 2 * p + 2, 1), pack_right)
        heads = g_turn[f, x, :, pl.ds(0, LANES)]
        pack_left = jnp.where(mine, pltpu.roll(heads, 2 * p, 1) if p else heads, pack_left)
    edge_right[...] = pack_right
    edge_left[...] = pack_left
    for copy in edges:
        copy.start()

    inv_radius = 1.0 / radius_of(0, cycles)
    angular = inv_radius * (1.0 / (12.0 * (2.0 * math.pi / total)))
    radial = inv_radius * (1.0 / 12.0)
    tail_row = lax.broadcasted_iota(jnp.int32, (8, width), 0)
    beyond = jnp.where(
        tail_row < 2, (tail_row.astype(F32) + (cycles + 0.5)) * (1.0 / (cycles - 0.5)), 0.0
    )
    for f, x in planes:
        g = g_turn[f, x]
        turn_term = 8.0 * (pltpu.roll(g, width - 1, 1) - pltpu.roll(g, 1, 1)) - (
            pltpu.roll(g, width - 2, 1) - pltpu.roll(g, 2, 1)
        )
        g = g_out[f, x]
        tall = cycles + 8
        g = jnp.concatenate([g, beyond * g[cycles - 1 :]], axis=0)
        out_term = (
            8.0 * (pltpu.roll(g, tall - 1, 0) - pltpu.roll(g, 1, 0))
            - (pltpu.roll(g, tall - 2, 0) - pltpu.roll(g, 2, 0))
        )[:cycles]
        change = -(turn_term * angular + out_term * radial)
        if f in (2, 3):
            change = change + rate[f, x]
        rate[f, x] = STEP_DT * change

    for copy in edges:
        copy.wait_recv()
    from_left = edge_from_left[...] - edge_right[...]
    from_right = edge_from_right[...] - edge_left[...]
    even = (edge_lane & 1) == 0
    scale = -STEP_DT * angular[:, :LANES]
    from_left = scale * jnp.where(
        even, from_left - 8.0 * pltpu.roll(from_left, LANES - 1, 1), from_left
    )
    from_right = scale * jnp.where(
        even, -from_right, 8.0 * pltpu.roll(from_right, 1, 1) - from_right
    )
    head, end = pl.ds(0, LANES), pl.ds((cells - 1) // LANES * LANES, LANES)
    end_lane = (cells - 2) % LANES
    ghost_row = lax.broadcasted_iota(jnp.int32, (8, width), 0)
    ghost_scale = -STEP_DT * radial[:8]
    for p, (f, x) in enumerate(planes):
        value = pltpu.roll(from_left, (LANES - 2 * p) % LANES, 1) if p else from_left
        rate[f, x, :, head] = rate[f, x, :, head] + jnp.where(edge_lane < 2, value, 0.0)
        value = pltpu.roll(from_right, (end_lane - 2 * p) % LANES, 1)
        mine = (edge_lane >= end_lane) & (edge_lane < end_lane + 2)
        rate[f, x, :, end] = rate[f, x, :, end] + jnp.where(mine, value, 0.0)
        tile = -ghost[f, x] if f in (2, 3) else ghost[f, x]
        inside = jnp.where(
            ghost_row == 0,
            pltpu.roll(tile, 7, 0) - 8.0 * tile,
            jnp.where(ghost_row == 1, pltpu.roll(tile, 1, 0), 0.0),
        )
        rate[f, x, pl.ds(0, 8), :] = rate[f, x, pl.ds(0, 8), :] + ghost_scale * inside

    for k in [CHUNKS] + list(range(CHUNKS)):
        for copy in crossings[k]:
            copy.wait_recv()
        rows = pieces[k]
        for f in range(fields):
            own = [fx_own[f, x, rows, :] for x in range(axial)]
            left = [fx_left[f, x, rows, :] for x in range(axial)]
            right = [fx_right[f, x, rows, :] for x in range(axial)]
            terms = (
                8.0 * (own[1] - left[1]) - (right[0] - left[0]),
                8.0 * (right[0] - own[0]) - (right[1] - left[1]),
            )
            for x, term in enumerate(terms):
                out[f, x, rows, :] = rate[f, x, rows, :] - (STEP_DT / 12.0) * term

    for pair in crossings:
        for copy in pair:
            copy.wait_send()
    for group in moments:
        for copy in group:
            copy.wait_send()
    for copy in edges:
        copy.wait_send()


def shards(state, start, modes):
    fields, axial, cells, cycles = state.shape
    inner = modes.shape[0]
    cfg = dict(plan(cells, lax.axis_size("azim")), cells=cells)
    width, depth = cfg["width"], cfg["depth"]
    turned = state.transpose(0, 1, 3, 2)
    if width != cells:
        turned = jnp.concatenate([turned] * (width // cells), axis=3)
    table = jnp.asarray(cfg["table"])
    full = (fields, axial, cycles, width)
    columns = 2 * fields * axial * inner // CHUNKS
    hbm = pl.BlockSpec(memory_space=pltpu.HBM)
    vmem = pl.BlockSpec(memory_space=pltpu.VMEM)
    peers = len(cfg["ranks"])
    step = pl.pallas_call(
        functools.partial(kernel, cfg),
        out_shape=jax.ShapeDtypeStruct(full, F32),
        in_specs=[hbm, hbm, hbm],
        out_specs=vmem,
        scratch_shapes=[
            pltpu.VMEM(full, F32),
            pltpu.VMEM((1, inner), jnp.int32),
            pltpu.VMEM(table.shape, BF16),
            pltpu.VMEM((inner, width), F32),
            pltpu.VMEM((inner, width), F32),
            pltpu.VMEM((CHUNKS, columns, width), BF16),
            pltpu.VMEM((CHUNKS, columns, width), BF16),
            pltpu.VMEM((CHUNKS, columns, width), F32),
            pltpu.VMEM((CHUNKS, depth, columns), F32),
            pltpu.VMEM((CHUNKS, depth, columns), F32),
        ]
        + [pltpu.VMEM(full, F32)] * 6
        + [pltpu.VMEM((cycles, LANES), F32)] * 4
        + [
            pltpu.VMEM((fields, axial, 8, width), F32),
            pltpu.SemaphoreType.DMA((4,)),
            pltpu.SemaphoreType.DMA((CHUNKS, peers)),
            pltpu.SemaphoreType.DMA((CHUNKS, peers)),
            pltpu.SemaphoreType.DMA((2, CHUNKS + 1)),
            pltpu.SemaphoreType.DMA((2, CHUNKS + 1)),
            pltpu.SemaphoreType.DMA((3,)),
            pltpu.SemaphoreType.DMA((3,)),
        ],
        compiler_params=pltpu.CompilerParams(
            collective_id=0, has_side_effects=True, vmem_limit_bytes=48 * 1024 * 1024
        ),
        name="jet_section",
    )(turned, modes.reshape(1, inner), table)
    if width != cells:
        step = step[..., :cells]
    return start + step.transpose(0, 1, 3, 2)


def solution(mesh):
    in_specs = (P(None, "axial", "azim", None), P(None, "axial", "azim", None), P())
    out_specs = P(None, "axial", "azim", None)
    return jax.shard_map(shards, mesh=mesh, in_specs=in_specs, out_specs=out_specs, check_vma=False)
```

time: 58.4 us -> 32.6 us (0.56)
  Pallas kernels: 48.3 us -> 28.1 us
  local copies, waits for them, and re-layouts: 8.68 us -> 2.85 us
    pallas_call x1, Pallas kernels: 48.3 us -> 28.1 us  [shards(): pl.pallas_call(functools.partial(kernel, cfg), out_shape=jax.ShapeDtypeSt...]
    unnamed x20 -> x8, local copies, waits for them, and re-layouts: 8.68 us -> 2.85 us
where the time goes in v1:
time: 32.6 us; the launch traced here: 32 us
  Pallas kernels  28.1 us (86%)
  local copies, waits for them, and re-layouts  2.85 us (9%)
  other arithmetic  1.07 us (3%)
    pallas_call x1, Pallas kernels, shards(): pl.pallas_call(functools.partial(kernel, cfg), out_shape=jax.ShapeDtypeSt...  28.1 us
    unnamed x8, local copies, waits for them, and re-layouts  2.85 us
    add x1, other arithmetic, shards(): return start + step.transpose(0, 1, 3, 2)  1.07 us

profile of v1, /device:TPU:1, one launch (start us, length us, event | category | flops | bytes accessed | tf_op | source)
XLA Modules:
  0.0 32.0 jit_solution(18419227816862132653)
XLA Ops:
  0.0 0.0 copy-start.2
  0.0 0.7 %copy-done.2 = s32[64]{0:T(128)S(1)} copy-done((s32[64]{0:T(128)S(1)}, s32[64]{0:T(128)}, u32[]{:S(2)}) %copy-start.2) | copy-done | bytes 280
  0.7 0.0 copy-start
  0.7 1.2 %copy-done = f32[5,2,256,96]{2,3,1,0:T(8,128)S(1)} copy-done((f32[5,2,256,96]{2,3,1,0:T(8,128)S(1)}, f32[5,2,256,96]{2,3,1,0:T(8,128)}, u32[]{:S(2)}) %copy-start) | copy-done | bytes 983064
  1.9 0.0 copy-start.1
  1.9 1.0 %copy-done.1 = bf16[720,256]{1,0:T(8,128)(2,1)S(1)} copy-done((bf16[720,256]{1,0:T(8,128)(2,1)S(1)}, bf16[720,256]{1,0:T(8,128)(2,1)}, u32[]{:S(2)}) %copy-start.1) | copy-done | bytes 368664
  2.8 0.0 copy-start.3
  2.8 28.1 %jet_section.1 = f32[5,2,96,256]{3,2,1,0:T(8,128)S(1)} custom-call(f32[5,2,96,256]{3,2,1,0:T(8,128)S(1)} %bitcast.4, s32[1,64]{1,0:T(1,128)S(1)} %bitcast.5, bf16[720,256]{1,0:T(8,128)(2,1)S(1)} %copy-done.1), custom_call_target="tpu_custom_call" | custom-call | tf_op jit(solution)/shard_map/jet_section/pallas_call | solution.py:407
  31.0 0.0 copy-done.3
  31.0 1.1 %bitcast_add_fusion = f32[5,2,256,96]{2,3,1,0:T(8,128)} fusion(f32[5,2,256,96]{2,3,1,0:T(8,128)S(1)} %copy-done.3, f32[5,2,96,256]{3,2,1,0:T(8,128)S(1)} %jet_section.1), kind=kLoop, calls=%fused_computation | loop fusion | flops 245760 | bytes 2949120 | tf_op jit(solution)/shard_map/add | solution.py:443
Async XLA Ops:
  0.0 0.7 %copy-start.2 = (s32[64]{0:T(128)S(1)}, s32[64]{0:T(128)}, u32[]{:S(2)}) copy-start(s32[64]{0:T(128)} %param.6) | copy-start | bytes 772
  0.7 1.2 %copy-start = (f32[5,2,256,96]{2,3,1,0:T(8,128)S(1)}, f32[5,2,256,96]{2,3,1,0:T(8,128)}, u32[]{:S(2)}) copy-start(f32[5,2,256,96]{2,3,1,0:T(8,128)} %param.4) | copy-start | bytes 2949124
  1.9 1.0 %copy-start.1 = (bf16[720,256]{1,0:T(8,128)(2,1)S(1)}, bf16[720,256]{1,0:T(8,128)(2,1)}, u32[]{:S(2)}) copy-start(bf16[720,256]{1,0:T(8,128)(2,1)} %constant.2.clone.table_hbm) | copy-start | bytes 1105924
  2.8 28.1 %copy-start.3 = (f32[5,2,256,96]{2,3,1,0:T(8,128)S(1)}, f32[5,2,256,96]{2,3,1,0:T(8,128)}, u32[]{:S(2)}) copy-start(f32[5,2,256,96]{2,3,1,0:T(8,128)} %param.5) | copy-start | bytes 2949124

commit v2 on v1

--- a/solution.py
+++ b/solution.py
@@ -63,6 +63,14 @@
     blank = np.zeros((stacked - 3 * depth, width), jnp.bfloat16)
     table = np.concatenate([*split_np(local), out_high, out_low, in_high, in_high, in_low, blank])
     return dict(width=width, depth=depth, stacked=stacked, starts=starts, ranks=ranks, table=table)
+
+
+def pieces_of(inner, cycles):
+    span = inner // CHUNKS
+    pieces = [(inner, cycles - inner)]
+    pieces += [(c * span, span) for c in range(CHUNKS - 1)]
+    half = span // 2
+    return pieces + [(inner - span, half), (inner - half, half // 2), (inner - half // 2, half // 2)]
 
 
 def split(values):
@@ -144,23 +152,22 @@
         )
 
     outer_rows, inner_rows = pl.ds(inner, cycles - inner), pl.ds(0, inner)
+    barrier = pltpu.get_barrier_semaphore()
+    peers = [x_right, x_left] + [z_at(offset) for offset in range(1, count)]
+    for device in peers:
+        pl.semaphore_signal(barrier, inc=1, device_id=device, device_id_type=MESH)
     loads = [
         pltpu.make_async_copy(modes_hbm, modes, load_sem.at[0]),
         pltpu.make_async_copy(
-            state_hbm.at[:, :, outer_rows], state.at[:, :, outer_rows], load_sem.at[1]
+            state_hbm.at[:, :, inner_rows], state.at[:, :, inner_rows], load_sem.at[1]
         ),
         pltpu.make_async_copy(
-            state_hbm.at[:, :, inner_rows], state.at[:, :, inner_rows], load_sem.at[2]
+            state_hbm.at[:, :, outer_rows], state.at[:, :, outer_rows], load_sem.at[2]
         ),
         pltpu.make_async_copy(table_hbm, table, load_sem.at[3]),
     ]
     for copy in loads:
         copy.start()
-
-    barrier = pltpu.get_barrier_semaphore()
-    peers = [z_at(offset) for offset in range(1, count)] + [x_right, x_left]
-    for device in peers:
-        pl.semaphore_signal(barrier, inc=1, device_id=device, device_id_type=MESH)
 
     moments = [
         [
@@ -172,18 +179,20 @@
         ]
         for c in range(CHUNKS)
     ]
-    pieces = [pl.ds(c * span, span) for c in range(CHUNKS)] + [outer_rows]
-    crossings = [
-        [
-            remote(
-                fx_own.at[:, :, rows], fx_left.at[:, :, rows], fx_send.at[0, k], fx_recv.at[0, k], x_right
-            ),
-            remote(
-                fx_own.at[:, :, rows], fx_right.at[:, :, rows], fx_send.at[1, k], fx_recv.at[1, k], x_left
-            ),
-        ]
-        for k, rows in enumerate(pieces)
-    ]
+    pieces = pieces_of(inner, cycles)
+    crossings = []
+    for k, (first, size) in enumerate(pieces):
+        rows = pl.ds(first, size)
+        source = state_hbm if first == inner else fx_own
+        crossings.append(
+            [
+                remote(
+                    source.at[:, :, rows], far_side.at[:, :, rows], fx_send.at[side, k],
+                    fx_recv.at[side, k], device,
+                )
+                for side, (far_side, device) in enumerate(((fx_left, x_right), (fx_right, x_left)))
+            ]
+        )
     edges = [
         remote(edge_right, edge_from_left, edge_send.at[0], edge_recv.at[0], z_at(1)),
         remote(edge_left, edge_from_right, edge_send.at[1], edge_recv.at[1], z_at(count - 1)),
@@ -191,6 +200,10 @@
             g_out.at[:, :, pl.ds(0, 8)], ghost, edge_send.at[2], edge_recv.at[2], z_at(count // 2)
         ),
     ]
+
+    pl.semaphore_wait(barrier, len(peers))
+    for copy in crossings[0]:
+        copy.start()
 
     loads[0].wait()
     kept = jnp.broadcast_to(modes[...], (inner, inner)).astype(F32)
@@ -212,15 +225,6 @@
             fx_own[f, x, rows, :] = part
 
     loads[1].wait()
-    for first in range(inner, cycles, BLOCK):
-        rows = pl.ds(first, BLOCK)
-        for x in range(axial):
-            axial_flux([state[f, x, rows, :] for f in range(fields)], x, rows)
-    pl.semaphore_wait(barrier, len(peers))
-    for copy in crossings[CHUNKS]:
-        copy.start()
-
-    loads[2].wait()
     loads[3].wait()
     out_table = table[pl.ds(2 * width, 2 * depth), :]
     contract_lanes = (((1,), (1,)), ((), ()))
@@ -249,6 +253,7 @@
     for c in range(CHUNKS):
         near[c] = mm(x_high[c], local_high) + mm(x_low[c], local_high) + mm(x_high[c], local_low)
 
+    ends = [(first + size, pair) for (first, size), pair in zip(pieces, crossings) if first != inner]
     in_table = table[pl.ds(2 * width + 2 * depth, stacked), :]
     for c in range(CHUNKS):
         for copy in moments[c]:
@@ -276,12 +281,15 @@
                     state[f, x, rows, :] = kept_value
                     values.append(kept_value)
                 axial_flux(values, x, rows)
-        for copy in crossings[c]:
-            copy.start()
+            for end, pair in ends:
+                if 0 < end - (c * span + first) <= BLOCK:
+                    for copy in pair:
+                        copy.start()
 
     radius_of = lambda first, size: (
         lax.broadcasted_iota(jnp.int32, (size, width), 0) + first
     ).astype(F32) + 0.5
+    loads[2].wait()
     for first in range(0, cycles, BLOCK):
         rows = pl.ds(first, BLOCK)
         radius = radius_of(first, BLOCK)
@@ -365,20 +373,32 @@
         )
         rate[f, x, pl.ds(0, 8), :] = rate[f, x, pl.ds(0, 8), :] + ghost_scale * inside
 
-    for k in [CHUNKS] + list(range(CHUNKS)):
-        for copy in crossings[k]:
+    def raw_flux(ref, x, rows):
+        values = [ref[f, x, rows, :] for f in range(fields)]
+        inverse = 1.0 / values[0]
+        return fluxes(values, 1, inverse, pressure_of(values, inverse))
+
+    for (begin, size), pair in zip(pieces, crossings):
+        for copy in pair:
             copy.wait_recv()
-        rows = pieces[k]
-        for f in range(fields):
-            own = [fx_own[f, x, rows, :] for x in range(axial)]
-            left = [fx_left[f, x, rows, :] for x in range(axial)]
-            right = [fx_right[f, x, rows, :] for x in range(axial)]
-            terms = (
-                8.0 * (own[1] - left[1]) - (right[0] - left[0]),
-                8.0 * (right[0] - own[0]) - (right[1] - left[1]),
-            )
-            for x, term in enumerate(terms):
-                out[f, x, rows, :] = rate[f, x, rows, :] - (STEP_DT / 12.0) * term
+        for first in range(begin, begin + size, 8):
+            rows = pl.ds(first, 8)
+            if begin == inner:
+                own, left, right = [
+                    [raw_flux(ref, x, rows) for x in range(axial)] for ref in (state, fx_left, fx_right)
+                ]
+            else:
+                own, left, right = [
+                    [[ref[f, x, rows, :] for f in range(fields)] for x in range(axial)]
+                    for ref in (fx_own, fx_left, fx_right)
+                ]
+            for f in range(fields):
+                terms = (
+                    8.0 * (own[1][f] - left[1][f]) - (right[0][f] - left[0][f]),
+                    8.0 * (right[0][f] - own[0][f]) - (right[1][f] - left[1][f]),
+                )
+                for x, term in enumerate(terms):
+                    out[f, x, rows, :] = rate[f, x, rows, :] - (STEP_DT / 12.0) * term
 
     for pair in crossings:
         for copy in pair:
@@ -398,12 +418,12 @@
     turned = state.transpose(0, 1, 3, 2)
     if width != cells:
         turned = jnp.concatenate([turned] * (width // cells), axis=3)
-    table = jnp.asarray(cfg["table"])
     full = (fields, axial, cycles, width)
     columns = 2 * fields * axial * inner // CHUNKS
     hbm = pl.BlockSpec(memory_space=pltpu.HBM)
     vmem = pl.BlockSpec(memory_space=pltpu.VMEM)
-    peers = len(cfg["ranks"])
+    peers, pieces = len(cfg["ranks"]), len(pieces_of(inner, cycles))
+    operands = (turned, modes.reshape(1, inner), jnp.asarray(cfg["table"]))
     step = pl.pallas_call(
         functools.partial(kernel, cfg),
         out_shape=jax.ShapeDtypeStruct(full, F32),
@@ -412,7 +432,7 @@
         scratch_shapes=[
             pltpu.VMEM(full, F32),
             pltpu.VMEM((1, inner), jnp.int32),
-            pltpu.VMEM(table.shape, BF16),
+            pltpu.VMEM(cfg["table"].shape, BF16),
             pltpu.VMEM((inner, width), F32),
             pltpu.VMEM((inner, width), F32),
             pltpu.VMEM((CHUNKS, columns, width), BF16),
@@ -428,8 +448,8 @@
             pltpu.SemaphoreType.DMA((4,)),
             pltpu.SemaphoreType.DMA((CHUNKS, peers)),
             pltpu.SemaphoreType.DMA((CHUNKS, peers)),
-            pltpu.SemaphoreType.DMA((2, CHUNKS + 1)),
-            pltpu.SemaphoreType.DMA((2, CHUNKS + 1)),
+            pltpu.SemaphoreType.DMA((2, pieces)),
+            pltpu.SemaphoreType.DMA((2, pieces)),
             pltpu.SemaphoreType.DMA((3,)),
             pltpu.SemaphoreType.DMA((3,)),
         ],
@@ -437,7 +457,7 @@
             collective_id=0, has_side_effects=True, vmem_limit_bytes=48 * 1024 * 1024
         ),
         name="jet_section",
-    )(turned, modes.reshape(1, inner), table)
+    )(*[pltpu.with_memory_space_constraint(operand, pltpu.HBM) for operand in operands])
     if width != cells:
         step = step[..., :cells]
     return start + step.transpose(0, 1, 3, 2)

time: 32.6 us -> 29.7 us (0.911)
  local copies, waits for them, and re-layouts: 2.85 us -> 0.01 us
    unnamed x8 -> x2, local copies, waits for them, and re-layouts: 2.85 us -> 0.01 us
where the time goes in v2:
time: 29.7 us; the launch traced here: 29.2 us
  Pallas kernels  28.1 us (95%)
  other arithmetic  1.07 us (4%)
    pallas_call x1, Pallas kernels, shards(): pl.pallas_call(functools.partial(kernel, cfg), out_shape=jax.ShapeDtypeSt...  28.1 us
    add x1, other arithmetic, shards(): return start + step.transpose(0, 1, 3, 2)  1.07 us

profile of v2, /device:TPU:1, one launch (start us, length us, event | category | flops | bytes accessed | tf_op | source)
XLA Modules:
  0.0 29.2 jit_solution(15084848354354604786)
XLA Ops:
  0.0 0.0 copy-start
  0.0 28.1 %jet_section.1 = f32[5,2,96,256]{3,2,1,0:T(8,128)S(1)} custom-call(f32[5,2,96,256]{3,2,1,0:T(8,128)} %bitcast.4, s32[1,64]{1,0:T(1,128)} %bitcast.5, bf16[720,256]{1,0:T(8,128)(2,1)} %constant.2.clone.table_hbm), custom_call_target="tpu_custom_call" | custom-call | tf_op jit(solution)/shard_map/jet_section/pallas_call | solution.py:427
  28.1 0.0 copy-done
  28.1 1.1 %bitcast_add_fusion = f32[5,2,256,96]{2,3,1,0:T(8,128)} fusion(f32[5,2,256,96]{2,3,1,0:T(8,128)S(1)} %copy-done, f32[5,2,96,256]{3,2,1,0:T(8,128)S(1)} %jet_section.1), kind=kLoop, calls=%fused_computation | loop fusion | flops 245760 | bytes 2949120 | tf_op jit(solution)/shard_map/add | solution.py:463
Async XLA Ops:
  0.0 28.1 %copy-start = (f32[5,2,256,96]{2,3,1,0:T(8,128)S(1)}, f32[5,2,256,96]{2,3,1,0:T(8,128)}, u32[]{:S(2)}) copy-start(f32[5,2,256,96]{2,3,1,0:T(8,128)} %param.5) | copy-start | bytes 2949124

commit v3 on v2

--- a/solution.py
+++ b/solution.py
@@ -13,6 +13,8 @@
 LANES = 128
 CHUNKS = 2
 BLOCK = 16
+MSTEP = 8
+TILE = 8
 FLOOR = 1e-9
 F32 = jnp.float32
 BF16 = jnp.bfloat16
@@ -62,14 +64,41 @@
     stacked = round_up(3 * depth, LANES)
     blank = np.zeros((stacked - 3 * depth, width), jnp.bfloat16)
     table = np.concatenate([*split_np(local), out_high, out_low, in_high, in_high, in_low, blank])
-    return dict(width=width, depth=depth, stacked=stacked, starts=starts, ranks=ranks, table=table)
+
+    def band(tile):
+        bound = min(2 * MSTEP * TILE * (tile + 1), total // 2)
+        waves = np.arange(1, bound)
+        phase = 2 * np.pi * ((where[:, None] * waves) % total) / total
+        scale = np.sqrt(2.0 / total)
+        columns = [np.full((cells, 1), 1.0 / np.sqrt(total)), scale * np.cos(phase), scale * np.sin(phase)]
+        left, values, _ = np.linalg.svd(np.concatenate(columns, axis=1))
+        return left, int(np.sum(values > FLOOR))
+
+    (first, low), (second, high) = band(0), band(1)
+    assert low + high <= width
+    low = min(cells, low + (width - low - high) // 2)
+    high = min(cells, width - low)
+    pack, unpack = [], []
+    for base, lanes in ((first[:, :low], (0, low)), (second[:, :high], (low, low + high))):
+        into = np.zeros((width, width))
+        into[:cells, lanes[0] : lanes[1]] = base
+        out_of = np.zeros((width, width))
+        out_of[lanes[0] : lanes[1]] = wide(base.T)
+        pack.append(split_np(into))
+        unpack.append(split_np(out_of))
+    bases = np.concatenate(
+        [pair[part] for pairs in (pack, unpack) for part in range(2) for pair in pairs]
+    )
+    return dict(
+        width=width, depth=depth, stacked=stacked, starts=starts, ranks=ranks, table=table, bases=bases
+    )
 
 
 def pieces_of(inner, cycles):
     span = inner // CHUNKS
-    pieces = [(inner, cycles - inner)]
-    pieces += [(c * span, span) for c in range(CHUNKS - 1)]
     half = span // 2
+    pieces = [(inner, cycles - inner), (2 * TILE, span - 2 * TILE), (0, 2 * TILE)]
+    pieces += [(c * span, span) for c in range(1, CHUNKS - 1)]
     return pieces + [(inner - span, half), (inner - half, half // 2), (inner - half // 2, half // 2)]
 
 
@@ -122,10 +151,10 @@
 
 def kernel(
     cfg,
-    state_hbm, modes_hbm, table_hbm, out,
-    state, modes, table, cosines, sines,
+    state_hbm, modes_hbm, table_hbm, bases_hbm, out,
+    state, modes, table, bases, cosines, sines,
     x_high, x_low, near, mom_own, mom_in,
-    fx_own, fx_left, fx_right, g_turn, g_out, rate,
+    fx_own, fx_left, fx_right, g_turn, g_out, rate, low_own, low_left, low_right,
     edge_right, edge_left, edge_from_left, edge_from_right, ghost,
     load_sem, mom_send, mom_recv, fx_send, fx_recv, edge_send, edge_recv,
 ):
@@ -165,6 +194,7 @@
             state_hbm.at[:, :, outer_rows], state.at[:, :, outer_rows], load_sem.at[2]
         ),
         pltpu.make_async_copy(table_hbm, table, load_sem.at[3]),
+        pltpu.make_async_copy(bases_hbm, bases, load_sem.at[4]),
     ]
     for copy in loads:
         copy.start()
@@ -183,14 +213,14 @@
     crossings = []
     for k, (first, size) in enumerate(pieces):
         rows = pl.ds(first, size)
-        source = state_hbm if first == inner else fx_own
+        source = (state_hbm if first == inner else fx_own).at[:, :, rows]
+        targets = fx_left.at[:, :, rows], fx_right.at[:, :, rows]
+        if first == 0:
+            source, targets = low_own, (low_left, low_right)
         crossings.append(
             [
-                remote(
-                    source.at[:, :, rows], far_side.at[:, :, rows], fx_send.at[side, k],
-                    fx_recv.at[side, k], device,
-                )
-                for side, (far_side, device) in enumerate(((fx_left, x_right), (fx_right, x_left)))
+                remote(source, target, fx_send.at[side, k], fx_recv.at[side, k], device)
+                for side, (target, device) in enumerate(zip(targets, (x_right, x_left)))
             ]
         )
     edges = [
@@ -253,7 +283,18 @@
     for c in range(CHUNKS):
         near[c] = mm(x_high[c], local_high) + mm(x_low[c], local_high) + mm(x_high[c], local_low)
 
-    ends = [(first + size, pair) for (first, size), pair in zip(pieces, crossings) if first != inner]
+    ends = [
+        (first + size, pair) for (first, size), pair in zip(pieces, crossings) if first not in (0, inner)
+    ]
+
+    def base(which, part, tile):
+        return bases[pl.ds((4 * which + 2 * part + tile) * width, width), :]
+
+    def change_basis(which, tile, high, low):
+        rows = high.shape[0]
+        both = mm(jnp.concatenate([high, low], axis=0), base(which, 0, tile))
+        return both[:rows] + both[rows:] + mm(high, base(which, 1, tile))
+
     in_table = table[pl.ds(2 * width + 2 * depth, stacked), :]
     for c in range(CHUNKS):
         for copy in moments[c]:
@@ -265,7 +306,7 @@
             parts.append(jnp.zeros((stacked - 3 * depth, high.shape[1]), F32))
         stack = jnp.concatenate(parts, axis=0).T.astype(BF16)
         near[c] = near[c] + mm(stack, in_table)
-        for first in range(0, span, BLOCK):
+        for first in reversed(range(0, span, BLOCK)) if c == 0 else range(0, span, BLOCK):
             rows = pl.ds(c * span + first, BLOCK)
             wave_sine, wave_cosine = sines[rows, :], cosines[rows, :]
             weight = share[c * span + first : c * span + first + BLOCK]
@@ -285,6 +326,17 @@
                 if 0 < end - (c * span + first) <= BLOCK:
                     for copy in pair:
                         copy.start()
+        if c == 0:
+            loads[4].wait()
+            packed = 0.0
+            for tile in range(2):
+                rows = pl.ds(tile * TILE, TILE)
+                value = jnp.concatenate([state[f, x, rows, :] for f, x in planes], axis=0)
+                packed = packed + change_basis(0, tile, *split(value))
+            for p, (f, x) in enumerate(planes):
+                low_own[f, x] = packed[p * TILE : (p + 1) * TILE]
+            for copy in crossings[2]:
+                copy.start()
 
     radius_of = lambda first, size: (
         lax.broadcasted_iota(jnp.int32, (size, width), 0) + first
@@ -381,9 +433,19 @@
     for (begin, size), pair in zip(pieces, crossings):
         for copy in pair:
             copy.wait_recv()
+        if begin == 0:
+            high, low = split(
+                jnp.concatenate([ref[f, x] for ref in (low_left, low_right) for f, x in planes], axis=0)
+            )
+            for tile in range(2):
+                value = change_basis(1, tile, high, low)
+                for side, ref in enumerate((fx_left, fx_right)):
+                    for p, (f, x) in enumerate(planes):
+                        row = (side * len(planes) + p) * TILE
+                        ref[f, x, pl.ds(tile * TILE, TILE), :] = value[row : row + TILE]
         for first in range(begin, begin + size, 8):
             rows = pl.ds(first, 8)
-            if begin == inner:
+            if begin in (0, inner):
                 own, left, right = [
                     [raw_flux(ref, x, rows) for x in range(axial)] for ref in (state, fx_left, fx_right)
                 ]
@@ -423,16 +485,17 @@
     hbm = pl.BlockSpec(memory_space=pltpu.HBM)
     vmem = pl.BlockSpec(memory_space=pltpu.VMEM)
     peers, pieces = len(cfg["ranks"]), len(pieces_of(inner, cycles))
-    operands = (turned, modes.reshape(1, inner), jnp.asarray(cfg["table"]))
+    tables = [jnp.asarray(cfg[name]) for name in ("table", "bases")]
+    operands = (turned, modes.reshape(1, inner), *tables)
     step = pl.pallas_call(
         functools.partial(kernel, cfg),
         out_shape=jax.ShapeDtypeStruct(full, F32),
-        in_specs=[hbm, hbm, hbm],
+        in_specs=[hbm] * 4,
         out_specs=vmem,
         scratch_shapes=[
             pltpu.VMEM(full, F32),
             pltpu.VMEM((1, inner), jnp.int32),
-            pltpu.VMEM(cfg["table"].shape, BF16),
+            *[pltpu.VMEM(table.shape, BF16) for table in tables],
             pltpu.VMEM((inner, width), F32),
             pltpu.VMEM((inner, width), F32),
             pltpu.VMEM((CHUNKS, columns, width), BF16),
@@ -442,10 +505,11 @@
             pltpu.VMEM((CHUNKS, depth, columns), F32),
         ]
         + [pltpu.VMEM(full, F32)] * 6
+        + [pltpu.VMEM((fields, axial, TILE, width), F32)] * 3
         + [pltpu.VMEM((cycles, LANES), F32)] * 4
         + [
             pltpu.VMEM((fields, axial, 8, width), F32),
-            pltpu.SemaphoreType.DMA((4,)),
+            pltpu.SemaphoreType.DMA((5,)),
             pltpu.SemaphoreType.DMA((CHUNKS, peers)),
             pltpu.SemaphoreType.DMA((CHUNKS, peers)),
             pltpu.SemaphoreType.DMA((2, pieces)),

time: 29.7 us -> 28 us (0.943)
  Pallas kernels: 28.1 us -> 26.4 us
    pallas_call x1, Pallas kernels: 28.1 us -> 26.4 us  [shards(): pl.pallas_call(functools.partial(kernel, cfg), out_shape=jax.ShapeDtypeSt...]
where the time goes in v3:
time: 28 us; the launch traced here: 27.5 us
  Pallas kernels  26.4 us (94%)
  other arithmetic  1.07 us (4%)
    pallas_call x1, Pallas kernels, shards(): pl.pallas_call(functools.partial(kernel, cfg), out_shape=jax.ShapeDtypeSt...  26.4 us
    add x1, other arithmetic, shards(): return start + step.transpose(0, 1, 3, 2)  1.07 us

profile of v3, /device:TPU:1, one launch (start us, length us, event | category | flops | bytes accessed | tf_op | source)
XLA Modules:
  0.0 27.5 jit_solution(12489154931688623383)
XLA Ops:
  0.0 0.0 copy-start
  0.0 26.4 %jet_section.1 = f32[5,2,96,256]{3,2,1,0:T(8,128)S(1)} custom-call(f32[5,2,96,256]{3,2,1,0:T(8,128)} %bitcast.4, s32[1,64]{1,0:T(1,128)} %bitcast.5, bf16[720,256]{1,0:T(8,128)(2,1)} %constant.4.clone.table_hbm, bf16[2048,256]{1,0:T(8,128)(2,1)} %constant.5.clone.bases_hbm), custom_call_target="tpu_custom_call" | custom-call | tf_op jit(solution)/shard_map/jet_section/pallas_call | solution.py:490
  26.4 0.0 copy-done
  26.4 1.1 %bitcast_add_fusion = f32[5,2,256,96]{2,3,1,0:T(8,128)} fusion(f32[5,2,256,96]{2,3,1,0:T(8,128)S(1)} %copy-done, f32[5,2,96,256]{3,2,1,0:T(8,128)S(1)} %jet_section.1), kind=kLoop, calls=%fused_computation | loop fusion | flops 245760 | bytes 2949120 | tf_op jit(solution)/shard_map/add | solution.py:527
Async XLA Ops:
  0.0 26.4 %copy-start = (f32[5,2,256,96]{2,3,1,0:T(8,128)S(1)}, f32[5,2,256,96]{2,3,1,0:T(8,128)}, u32[]{:S(2)}) copy-start(f32[5,2,256,96]{2,3,1,0:T(8,128)} %param.6) | copy-start | bytes 2949124

commit v4 on v3

--- a/solution.py
+++ b/solution.py
@@ -182,9 +182,17 @@
 
     outer_rows, inner_rows = pl.ds(inner, cycles - inner), pl.ds(0, inner)
     barrier = pltpu.get_barrier_semaphore()
-    peers = [x_right, x_left] + [z_at(offset) for offset in range(1, count)]
-    for device in peers:
+    leads = d == 0
+
+    def greet(device):
         pl.semaphore_signal(barrier, inc=1, device_id=device, device_id_type=MESH)
+
+    for device in (x_right, x_left):
+        greet(device)
+    for offset in range(1, count):
+        pl.when(jnp.logical_not(leads) & (z_at(offset)["azim"] != 0))(
+            functools.partial(greet, z_at(offset))
+        )
     loads = [
         pltpu.make_async_copy(modes_hbm, modes, load_sem.at[0]),
         pltpu.make_async_copy(
@@ -231,9 +239,11 @@
         ),
     ]
 
-    pl.semaphore_wait(barrier, len(peers))
+    pl.semaphore_wait(barrier, jnp.where(leads, 2, count + 1))
     for copy in crossings[0]:
         copy.start()
+    for offset in range(1, count):
+        pl.when(leads | (z_at(offset)["azim"] == 0))(functools.partial(greet, z_at(offset)))
 
     loads[0].wait()
     kept = jnp.broadcast_to(modes[...], (inner, inner)).astype(F32)
@@ -276,6 +286,12 @@
             mom_own[c, pl.ds(starts[k], ranks[k]), :] = (
                 sums[starts[k] : starts[k] + ranks[k]] * wrapped
             )
+        if c == 0:
+
+            @pl.when(leads)
+            def _():
+                pl.semaphore_wait(barrier, count - 1)
+
         for copy in moments[c]:
             copy.start()
 

time: 28 us -> 25.8 us (0.921)
  the two profiles are of different devices: /device:TPU:1 before, /device:TPU:9 now
where the time goes in v4:
time: 25.8 us; the launch traced here: 25.7 us
  Pallas kernels  24.6 us (95%)
  other arithmetic  1.07 us (4%)
    pallas_call x1, Pallas kernels, shards(): pl.pallas_call(functools.partial(kernel, cfg), out_shape=jax.ShapeDtypeSt...  24.6 us
    add x1, other arithmetic, shards(): return start + step.transpose(0, 1, 3, 2)  1.07 us

profile of v4, /device:TPU:9, one launch (start us, length us, event | category | flops | bytes accessed | tf_op | source)
XLA Modules:
  0.0 25.7 jit_solution(3291581688002115325)
XLA Ops:
  0.0 0.0 copy-start
  0.0 24.6 %jet_section.1 = f32[5,2,96,256]{3,2,1,0:T(8,128)S(1)} custom-call(f32[5,2,96,256]{3,2,1,0:T(8,128)} %bitcast.4, s32[1,64]{1,0:T(1,128)} %bitcast.5, bf16[720,256]{1,0:T(8,128)(2,1)} %constant.4.clone.table_hbm, bf16[2048,256]{1,0:T(8,128)(2,1)} %constant.5.clone.bases_hbm), custom_call_target="tpu_custom_call" | custom-call | tf_op jit(solution)/shard_map/jet_section/pallas_call | solution.py:506
  24.6 0.0 copy-done
  24.6 1.1 %bitcast_add_fusion = f32[5,2,256,96]{2,3,1,0:T(8,128)} fusion(f32[5,2,256,96]{2,3,1,0:T(8,128)S(1)} %copy-done, f32[5,2,96,256]{3,2,1,0:T(8,128)S(1)} %jet_section.1), kind=kLoop, calls=%fused_computation | loop fusion | flops 245760 | bytes 2949120 | tf_op jit(solution)/shard_map/add | solution.py:543
Async XLA Ops:
  0.0 24.6 %copy-start = (f32[5,2,256,96]{2,3,1,0:T(8,128)S(1)}, f32[5,2,256,96]{2,3,1,0:T(8,128)}, u32[]{:S(2)}) copy-start(f32[5,2,256,96]{2,3,1,0:T(8,128)} %param.6) | copy-start | bytes 2949124

commit v5 on v4

--- a/solution.py
+++ b/solution.py
@@ -15,6 +15,9 @@
 BLOCK = 16
 MSTEP = 8
 TILE = 8
+GROUP = 4
+PACKED = 6
+CUT = 1e-6
 FLOOR = 1e-9
 F32 = jnp.float32
 BF16 = jnp.bfloat16
@@ -65,30 +68,28 @@
     blank = np.zeros((stacked - 3 * depth, width), jnp.bfloat16)
     table = np.concatenate([*split_np(local), out_high, out_low, in_high, in_high, in_low, blank])
 
-    def band(tile):
-        bound = min(2 * MSTEP * TILE * (tile + 1), total // 2)
+    def band(group):
+        bound = min(2 * MSTEP * GROUP * (group + 1), total // 2)
         waves = np.arange(1, bound)
         phase = 2 * np.pi * ((where[:, None] * waves) % total) / total
         scale = np.sqrt(2.0 / total)
         columns = [np.full((cells, 1), 1.0 / np.sqrt(total)), scale * np.cos(phase), scale * np.sin(phase)]
         left, values, _ = np.linalg.svd(np.concatenate(columns, axis=1))
-        return left, int(np.sum(values > FLOOR))
-
-    (first, low), (second, high) = band(0), band(1)
-    assert low + high <= width
-    low = min(cells, low + (width - low - high) // 2)
-    high = min(cells, width - low)
-    pack, unpack = [], []
-    for base, lanes in ((first[:, :low], (0, low)), (second[:, :high], (low, low + high))):
-        into = np.zeros((width, width))
-        into[:cells, lanes[0] : lanes[1]] = base
-        out_of = np.zeros((width, width))
-        out_of[lanes[0] : lanes[1]] = wide(base.T)
-        pack.append(split_np(into))
-        unpack.append(split_np(out_of))
-    bases = np.concatenate(
-        [pair[part] for pairs in (pack, unpack) for part in range(2) for pair in pairs]
-    )
+        return left, np.append(values, np.zeros(cells + 1 - len(values)))
+
+    blocks = [None] * PACKED
+    for low in range(PACKED // 2):
+        high = PACKED - 1 - low
+        (first, first_values), (second, second_values) = band(low), band(high)
+        sizes = range(max(width - cells, 0), min(cells, width) + 1)
+        size = min(sizes, key=lambda n: max(first_values[n], second_values[width - n]))
+        assert max(first_values[size], second_values[width - size]) < CUT
+        blocks[low] = np.zeros((width, width))
+        blocks[low][:cells, :size] = first[:, :size]
+        blocks[high] = np.zeros((width, width))
+        blocks[high][:cells, size:] = second[:, : width - size]
+    halves = [split_np(block) for block in blocks]
+    bases = np.concatenate([pair[part] for part in range(2) for pair in halves])
     return dict(
         width=width, depth=depth, stacked=stacked, starts=starts, ranks=ranks, table=table, bases=bases
     )
@@ -97,7 +98,8 @@
 def pieces_of(inner, cycles):
     span = inner // CHUNKS
     half = span // 2
-    pieces = [(inner, cycles - inner), (2 * TILE, span - 2 * TILE), (0, 2 * TILE)]
+    packed = PACKED * GROUP
+    pieces = [(inner, cycles - inner), (packed, span - packed), (0, packed)]
     pieces += [(c * span, span) for c in range(1, CHUNKS - 1)]
     return pieces + [(inner - span, half), (inner - half, half // 2), (inner - half // 2, half // 2)]
 
@@ -109,6 +111,10 @@
 
 def mm(a, b):
     return jnp.dot(a, b, preferred_element_type=F32)
+
+
+def mm_lanes(a, b):
+    return lax.dot_general(a, b, (((1,), (1,)), ((), ())), preferred_element_type=F32)
 
 
 def pressure_of(values, inverse):
@@ -267,7 +273,6 @@
     loads[1].wait()
     loads[3].wait()
     out_table = table[pl.ds(2 * width, 2 * depth), :]
-    contract_lanes = (((1,), (1,)), ((), ()))
     for c in range(CHUNKS):
         rows = pl.ds(c * span, span)
         for p, (f, x) in enumerate(planes):
@@ -277,9 +282,7 @@
                 slot = pl.ds((2 * p + part) * span, span)
                 x_high[c, slot, :] = high
                 x_low[c, slot, :] = low
-        sums = lax.dot_general(
-            out_table, x_high[c], contract_lanes, preferred_element_type=F32
-        ) + lax.dot_general(out_table, x_low[c], contract_lanes, preferred_element_type=F32)
+        sums = mm_lanes(out_table, x_high[c]) + mm_lanes(out_table, x_low[c])
         sums = sums[:depth] + sums[depth:]
         for k in range(len(ranks)):
             wrapped = (1 - 2 * ((d + k + 1) // count)).astype(F32)
@@ -303,13 +306,21 @@
         (first + size, pair) for (first, size), pair in zip(pieces, crossings) if first not in (0, inner)
     ]
 
-    def base(which, part, tile):
-        return bases[pl.ds((4 * which + 2 * part + tile) * width, width), :]
-
-    def change_basis(which, tile, high, low):
-        rows = high.shape[0]
-        both = mm(jnp.concatenate([high, low], axis=0), base(which, 0, tile))
-        return both[:rows] + both[rows:] + mm(high, base(which, 1, tile))
+    def into_basis(group, high, low):
+        rows, at = high.shape[0], lambda part: pl.ds((PACKED * part + group) * width, width)
+        both = mm(jnp.concatenate([high, low], axis=0), bases[at(0), :])
+        return both[:rows] + both[rows:] + mm(high, bases[at(1), :])
+
+    def from_basis(group, high, low):
+        rows, at = high.shape[0], lambda part: pl.ds((PACKED * part + group) * width, width)
+        both = mm_lanes(jnp.concatenate([high, low], axis=0), bases[at(0), :])
+        return both[:rows] + both[rows:] + mm_lanes(high, bases[at(1), :])
+
+    def upper(rows):
+        return (lax.broadcasted_iota(jnp.int32, (rows, width), 0) & GROUP) == 0
+
+    def swapped(tile):
+        return pltpu.roll(tile, GROUP, 0)
 
     in_table = table[pl.ds(2 * width + 2 * depth, stacked), :]
     for c in range(CHUNKS):
@@ -344,13 +355,24 @@
                         copy.start()
         if c == 0:
             loads[4].wait()
-            packed = 0.0
-            for tile in range(2):
-                rows = pl.ds(tile * TILE, TILE)
-                value = jnp.concatenate([state[f, x, rows, :] for f, x in planes], axis=0)
-                packed = packed + change_basis(0, tile, *split(value))
+            tiles = [
+                [state[f, x, pl.ds(TILE * t, TILE), :] for f, x in planes] for t in range(PACKED * GROUP // TILE)
+            ]
+            first, middle, last = [split(jnp.concatenate(tile, axis=0)) for tile in tiles]
+            middle_swapped, last_swapped = [
+                split(jnp.concatenate([swapped(part) for part in tile], axis=0)) for tile in tiles[1:]
+            ]
+            outside = jnp.where(
+                upper(len(planes) * TILE),
+                into_basis(0, *first) + into_basis(5, *last_swapped),
+                into_basis(1, *first) + into_basis(4, *last_swapped),
+            )
+            inside = into_basis(2, *middle) + into_basis(3, *middle_swapped)
             for p, (f, x) in enumerate(planes):
-                low_own[f, x] = packed[p * TILE : (p + 1) * TILE]
+                low_own[f, x] = outside[p * TILE : (p + 1) * TILE]
+            for f in range(fields):
+                even, odd = [inside[p * TILE : (p + 1) * TILE] for p in (2 * f, 2 * f + 1)]
+                low_own[f, axial] = jnp.where(upper(TILE), even, swapped(odd))
             for copy in crossings[2]:
                 copy.start()
 
@@ -450,15 +472,22 @@
         for copy in pair:
             copy.wait_recv()
         if begin == 0:
-            high, low = split(
-                jnp.concatenate([ref[f, x] for ref in (low_left, low_right) for f, x in planes], axis=0)
-            )
-            for tile in range(2):
-                value = change_basis(1, tile, high, low)
-                for side, ref in enumerate((fx_left, fx_right)):
-                    for p, (f, x) in enumerate(planes):
-                        row = (side * len(planes) + p) * TILE
-                        ref[f, x, pl.ds(tile * TILE, TILE), :] = value[row : row + TILE]
+            sides = (low_left, low_right)
+            outside = split(jnp.concatenate([ref[f, x] for ref in sides for f, x in planes], axis=0))
+            inside = split(jnp.concatenate([ref[f, axial] for ref in sides for f in range(fields)], axis=0))
+            half = upper(2 * len(planes) * TILE)
+            head = jnp.where(half, from_basis(0, *outside), from_basis(1, *outside))
+            last = jnp.where(half, from_basis(5, *outside), from_basis(4, *outside))
+            second, third = from_basis(2, *inside), from_basis(3, *inside)
+            for side, ref in enumerate((fx_left, fx_right)):
+                for p, (f, x) in enumerate(planes):
+                    row = (side * len(planes) + p) * TILE
+                    ref[f, x, pl.ds(0, TILE), :] = head[row : row + TILE]
+                    ref[f, x, pl.ds(2 * TILE, TILE), :] = swapped(last[row : row + TILE])
+                    row = (side * fields + f) * TILE
+                    early, late = second[row : row + TILE], third[row : row + TILE]
+                    early, late = (early, swapped(late)) if x == 0 else (swapped(early), late)
+                    ref[f, x, pl.ds(TILE, TILE), :] = jnp.where(upper(TILE), early, late)
         for first in range(begin, begin + size, 8):
             rows = pl.ds(first, 8)
             if begin in (0, inner):
@@ -521,7 +550,7 @@
             pltpu.VMEM((CHUNKS, depth, columns), F32),
         ]
         + [pltpu.VMEM(full, F32)] * 6
-        + [pltpu.VMEM((fields, axial, TILE, width), F32)] * 3
+        + [pltpu.VMEM((fields, axial + 1, TILE, width), F32)] * 3
         + [pltpu.VMEM((cycles, LANES), F32)] * 4
         + [
             pltpu.VMEM((fields, axial, 8, width), F32),

time: 25.8 us -> 24.9 us (0.965)
  Pallas kernels: 24.6 us -> 23.7 us
    pallas_call x1, Pallas kernels: 24.6 us -> 23.7 us  [shards(): pl.pallas_call(functools.partial(kernel, cfg), out_shape=jax.ShapeDtypeSt...]
where the time goes in v5:
time: 24.9 us; the launch traced here: 24.8 us
  Pallas kernels  23.7 us (95%)
  other arithmetic  1.07 us (4%)
    pallas_call x1, Pallas kernels, shards(): pl.pallas_call(functools.partial(kernel, cfg), out_shape=jax.ShapeDtypeSt...  23.7 us
    add x1, other arithmetic, shards(): return start + step.transpose(0, 1, 3, 2)  1.07 us

profile of v5, /device:TPU:9, one launch (start us, length us, event | category | flops | bytes accessed | tf_op | source)
XLA Modules:
  0.0 24.8 jit_solution(12037844486735591)
XLA Ops:
  0.0 0.0 copy-start
  0.0 23.7 %jet_section.1 = f32[5,2,96,256]{3,2,1,0:T(8,128)S(1)} custom-call(f32[5,2,96,256]{3,2,1,0:T(8,128)} %bitcast.4, s32[1,64]{1,0:T(1,128)} %bitcast.5, bf16[720,256]{1,0:T(8,128)(2,1)} %constant.4.clone.table_hbm, bf16[3072,256]{1,0:T(8,128)(2,1)} %constant.5.clone.bases_hbm), custom_call_target="tpu_custom_call" | custom-call | tf_op jit(solution)/shard_map/jet_section/pallas_call | solution.py:535
  23.7 0.0 copy-done
  23.7 1.1 %bitcast_add_fusion = f32[5,2,256,96]{2,3,1,0:T(8,128)} fusion(f32[5,2,256,96]{2,3,1,0:T(8,128)S(1)} %copy-done, f32[5,2,96,256]{3,2,1,0:T(8,128)S(1)} %jet_section.1), kind=kLoop, calls=%fused_computation | loop fusion | flops 245760 | bytes 2949120 | tf_op jit(solution)/shard_map/add | solution.py:572
Async XLA Ops:
  0.0 23.7 %copy-start = (f32[5,2,256,96]{2,3,1,0:T(8,128)S(1)}, f32[5,2,256,96]{2,3,1,0:T(8,128)}, u32[]{:S(2)}) copy-start(f32[5,2,256,96]{2,3,1,0:T(8,128)} %param.6) | copy-start | bytes 2949124

commit v6 on v5

--- a/solution.py
+++ b/solution.py
@@ -157,8 +157,8 @@
 
 def kernel(
     cfg,
-    state_hbm, modes_hbm, table_hbm, bases_hbm, out,
-    state, modes, table, bases, cosines, sines,
+    state_hbm, start_hbm, modes_hbm, table_hbm, bases_hbm, out,
+    state, begun, modes, table, bases, cosines, sines,
     x_high, x_low, near, mom_own, mom_in,
     fx_own, fx_left, fx_right, g_turn, g_out, rate, low_own, low_left, low_right,
     edge_right, edge_left, edge_from_left, edge_from_right, ghost,
@@ -209,6 +209,7 @@
         ),
         pltpu.make_async_copy(table_hbm, table, load_sem.at[3]),
         pltpu.make_async_copy(bases_hbm, bases, load_sem.at[4]),
+        pltpu.make_async_copy(start_hbm, begun, load_sem.at[5]),
     ]
     for copy in loads:
         copy.start()
@@ -409,6 +410,7 @@
     for copy in edges:
         copy.start()
 
+    loads[5].wait()
     inv_radius = 1.0 / radius_of(0, cycles)
     angular = inv_radius * (1.0 / (12.0 * (2.0 * math.pi / total)))
     radial = inv_radius * (1.0 / 12.0)
@@ -431,7 +433,7 @@
         change = -(turn_term * angular + out_term * radial)
         if f in (2, 3):
             change = change + rate[f, x]
-        rate[f, x] = STEP_DT * change
+        rate[f, x] = begun[f, x] + STEP_DT * change
 
     for copy in edges:
         copy.wait_recv()
@@ -522,22 +524,24 @@
     inner = modes.shape[0]
     cfg = dict(plan(cells, lax.axis_size("azim")), cells=cells)
     width, depth = cfg["width"], cfg["depth"]
-    turned = state.transpose(0, 1, 3, 2)
-    if width != cells:
-        turned = jnp.concatenate([turned] * (width // cells), axis=3)
+    turned, begun = [
+        jnp.concatenate([values.transpose(0, 1, 3, 2)] * (width // cells), axis=3)
+        for values in (state, start)
+    ]
     full = (fields, axial, cycles, width)
     columns = 2 * fields * axial * inner // CHUNKS
     hbm = pl.BlockSpec(memory_space=pltpu.HBM)
     vmem = pl.BlockSpec(memory_space=pltpu.VMEM)
     peers, pieces = len(cfg["ranks"]), len(pieces_of(inner, cycles))
     tables = [jnp.asarray(cfg[name]) for name in ("table", "bases")]
-    operands = (turned, modes.reshape(1, inner), *tables)
+    operands = (turned, begun, modes.reshape(1, inner), *tables)
     step = pl.pallas_call(
         functools.partial(kernel, cfg),
         out_shape=jax.ShapeDtypeStruct(full, F32),
-        in_specs=[hbm] * 4,
+        in_specs=[hbm] * 5,
         out_specs=vmem,
         scratch_shapes=[
+            pltpu.VMEM(full, F32),
             pltpu.VMEM(full, F32),
             pltpu.VMEM((1, inner), jnp.int32),
             *[pltpu.VMEM(table.shape, BF16) for table in tables],
@@ -554,7 +558,7 @@
         + [pltpu.VMEM((cycles, LANES), F32)] * 4
         + [
             pltpu.VMEM((fields, axial, 8, width), F32),
-            pltpu.SemaphoreType.DMA((5,)),
+            pltpu.SemaphoreType.DMA((6,)),
             pltpu.SemaphoreType.DMA((CHUNKS, peers)),
             pltpu.SemaphoreType.DMA((CHUNKS, peers)),
             pltpu.SemaphoreType.DMA((2, pieces)),
@@ -567,9 +571,7 @@
         ),
         name="jet_section",
     )(*[pltpu.with_memory_space_constraint(operand, pltpu.HBM) for operand in operands])
-    if width != cells:
-        step = step[..., :cells]
-    return start + step.transpose(0, 1, 3, 2)
+    return step[..., :cells].transpose(0, 1, 3, 2)
 
 
 def solution(mesh):

time: 24.9 us -> 24.8 us (level)
  other arithmetic: 1.07 us -> 0 us
  local copies, waits for them, and re-layouts: 0.01 us -> 0.95 us
    add x1 -> x0, other arithmetic: 1.07 us -> none  [shards(): return start + step.transpose(0, 1, 3, 2)]
    unnamed x2 -> x1, local copies, waits for them, and re-layouts: 0.01 us -> 0.95 us
where the time goes in v6:
time: 24.8 us; the launch traced here: 24.7 us
  Pallas kernels  23.7 us (96%)
  local copies, waits for them, and re-layouts  0.95 us (4%)
    pallas_call x1, Pallas kernels, shards(): pl.pallas_call(functools.partial(kernel, cfg), out_shape=jax.ShapeDtypeSt...  23.7 us
    unnamed x1, local copies, waits for them, and re-layouts  0.95 us

profile of v6, /device:TPU:9, one launch (start us, length us, event | category | flops | bytes accessed | tf_op | source)
XLA Modules:
  0.0 24.7 jit_solution(1074276792131671923)
XLA Ops:
  0.0 23.7 %jet_section.1 = f32[5,2,96,256]{3,2,1,0:T(8,128)S(1)} custom-call(f32[5,2,96,256]{3,2,1,0:T(8,128)} %bitcast.5, f32[5,2,96,256]{3,2,1,0:T(8,128)} %bitcast.6, s32[1,64]{1,0:T(1,128)} %bitcast.7, bf16[720,256]{1,0:T(8,128)(2,1)} %constant.4.clone.table_hbm, bf16[3072,256]{1,0:T(8,128)(2,1)} %constant.5.clone.bases_hbm), custom_call_target="tpu_custom_call" | custom-call | tf_op jit(solution)/shard_map/jet_section/pallas_call | solution.py:538
  23.7 0.9 %copy.7 = f32[5,2,256,96]{2,3,1,0:T(8,128)} copy(f32[5,2,256,96]{2,3,1,0:T(8,128)S(1)} %bitcast.4) | data formatting | bytes 1966080

commit v7 on v6

--- a/solution.py
+++ b/solution.py
@@ -18,6 +18,7 @@
 GROUP = 4
 PACKED = 6
 CUT = 1e-6
+LEVELS = 3
 FLOOR = 1e-9
 F32 = jnp.float32
 BF16 = jnp.bfloat16
@@ -188,17 +189,20 @@
 
     outer_rows, inner_rows = pl.ds(inner, cycles - inner), pl.ds(0, inner)
     barrier = pltpu.get_barrier_semaphore()
-    leads = d == 0
+    level = jnp.minimum(d, LEVELS - 1)
+    level_mates = jnp.where(level == LEVELS - 1, count - LEVELS, 0)
+    azim_peers = [z_at(offset) for offset in range(1, count)]
+    peer_levels = [jnp.minimum(device["azim"], LEVELS - 1) for device in azim_peers]
+    is_mate = [peer_level == level for peer_level in peer_levels]
+    is_later = [peer_level > level for peer_level in peer_levels]
 
     def greet(device):
         pl.semaphore_signal(barrier, inc=1, device_id=device, device_id_type=MESH)
 
     for device in (x_right, x_left):
         greet(device)
-    for offset in range(1, count):
-        pl.when(jnp.logical_not(leads) & (z_at(offset)["azim"] != 0))(
-            functools.partial(greet, z_at(offset))
-        )
+    for device, mate in zip(azim_peers, is_mate):
+        pl.when(mate)(functools.partial(greet, device))
     loads = [
         pltpu.make_async_copy(modes_hbm, modes, load_sem.at[0]),
         pltpu.make_async_copy(
@@ -246,11 +250,11 @@
         ),
     ]
 
-    pl.semaphore_wait(barrier, jnp.where(leads, 2, count + 1))
+    pl.semaphore_wait(barrier, 2 + level + level_mates)
     for copy in crossings[0]:
         copy.start()
-    for offset in range(1, count):
-        pl.when(leads | (z_at(offset)["azim"] == 0))(functools.partial(greet, z_at(offset)))
+    for device, mate in zip(azim_peers, is_mate):
+        pl.when(jnp.logical_not(mate))(functools.partial(greet, device))
 
     loads[0].wait()
     kept = jnp.broadcast_to(modes[...], (inner, inner)).astype(F32)
@@ -291,13 +295,18 @@
                 sums[starts[k] : starts[k] + ranks[k]] * wrapped
             )
         if c == 0:
-
-            @pl.when(leads)
+            for copy, later in zip(moments[c], is_later):
+                pl.when(jnp.logical_not(later))(copy.start)
+
+            @pl.when(level < LEVELS - 1)
             def _():
-                pl.semaphore_wait(barrier, count - 1)
-
-        for copy in moments[c]:
-            copy.start()
+                pl.semaphore_wait(barrier, count - 1 - level)
+
+            for copy, later in zip(moments[c], is_later):
+                pl.when(later)(copy.start)
+        else:
+            for copy in moments[c]:
+                copy.start()
 
     local_high, local_low = table[pl.ds(0, width), :], table[pl.ds(width, width), :]
     for c in range(CHUNKS):

time: 24.8 us -> 24.5 us (0.988)
  the two profiles are of different devices: /device:TPU:9 before, /device:TPU:1 now
where the time goes in v7:
time: 24.5 us; the launch traced here: 24.1 us
  Pallas kernels  23.2 us (95%)
  local copies, waits for them, and re-layouts  0.95 us (4%)
    pallas_call x1, Pallas kernels, shards(): pl.pallas_call(functools.partial(kernel, cfg), out_shape=jax.ShapeDtypeSt...  23.2 us
    unnamed x1, local copies, waits for them, and re-layouts  0.95 us

profile of v7, /device:TPU:1, one launch (start us, length us, event | category | flops | bytes accessed | tf_op | source)
XLA Modules:
  0.0 24.1 jit_solution(14485103011385049865)
XLA Ops:
  0.0 23.2 %jet_section.1 = f32[5,2,96,256]{3,2,1,0:T(8,128)S(1)} custom-call(f32[5,2,96,256]{3,2,1,0:T(8,128)} %bitcast.5, f32[5,2,96,256]{3,2,1,0:T(8,128)} %bitcast.6, s32[1,64]{1,0:T(1,128)} %bitcast.7, bf16[720,256]{1,0:T(8,128)(2,1)} %constant.4.clone.table_hbm, bf16[3072,256]{1,0:T(8,128)(2,1)} %constant.5.clone.bases_hbm), custom_call_target="tpu_custom_call" | custom-call | tf_op jit(solution)/shard_map/jet_section/pallas_call | solution.py:547
  23.2 0.9 %copy.7 = f32[5,2,256,96]{2,3,1,0:T(8,128)} copy(f32[5,2,256,96]{2,3,1,0:T(8,128)S(1)} %bitcast.4) | data formatting | bytes 1966080

commit v8 on v7

--- a/solution.py
+++ b/solution.py
@@ -163,7 +163,7 @@
     x_high, x_low, near, mom_own, mom_in,
     fx_own, fx_left, fx_right, g_turn, g_out, rate, low_own, low_left, low_right,
     edge_right, edge_left, edge_from_left, edge_from_right, ghost,
-    load_sem, mom_send, mom_recv, fx_send, fx_recv, edge_send, edge_recv,
+    load_sem, mom_send, mom_recv, fx_send, fx_recv, edge_send, edge_recv, answered,
 ):
     fields, axial, cycles, width = state.shape
     cells, inner = cfg["cells"], modes.shape[1]
@@ -193,16 +193,16 @@
     level_mates = jnp.where(level == LEVELS - 1, count - LEVELS, 0)
     azim_peers = [z_at(offset) for offset in range(1, count)]
     peer_levels = [jnp.minimum(device["azim"], LEVELS - 1) for device in azim_peers]
-    is_mate = [peer_level == level for peer_level in peer_levels]
+    is_earlier = [peer_level < level for peer_level in peer_levels]
     is_later = [peer_level > level for peer_level in peer_levels]
 
-    def greet(device):
-        pl.semaphore_signal(barrier, inc=1, device_id=device, device_id_type=MESH)
+    def greet(device, semaphore=barrier):
+        pl.semaphore_signal(semaphore, inc=1, device_id=device, device_id_type=MESH)
 
     for device in (x_right, x_left):
         greet(device)
-    for device, mate in zip(azim_peers, is_mate):
-        pl.when(mate)(functools.partial(greet, device))
+    for device, earlier in zip(azim_peers, is_earlier):
+        pl.when(jnp.logical_not(earlier))(functools.partial(greet, device))
     loads = [
         pltpu.make_async_copy(modes_hbm, modes, load_sem.at[0]),
         pltpu.make_async_copy(
@@ -253,8 +253,8 @@
     pl.semaphore_wait(barrier, 2 + level + level_mates)
     for copy in crossings[0]:
         copy.start()
-    for device, mate in zip(azim_peers, is_mate):
-        pl.when(jnp.logical_not(mate))(functools.partial(greet, device))
+    for device, earlier in zip(azim_peers, is_earlier):
+        pl.when(earlier)(functools.partial(greet, device, answered))
 
     loads[0].wait()
     kept = jnp.broadcast_to(modes[...], (inner, inner)).astype(F32)
@@ -300,7 +300,7 @@
 
             @pl.when(level < LEVELS - 1)
             def _():
-                pl.semaphore_wait(barrier, count - 1 - level)
+                pl.semaphore_wait(answered, count - 1 - level)
 
             for copy, later in zip(moments[c], is_later):
                 pl.when(later)(copy.start)
@@ -574,6 +574,7 @@
             pltpu.SemaphoreType.DMA((2, pieces)),
             pltpu.SemaphoreType.DMA((3,)),
             pltpu.SemaphoreType.DMA((3,)),
+            pltpu.SemaphoreType.REGULAR,
         ],
         compiler_params=pltpu.CompilerParams(
             collective_id=0, has_side_effects=True, vmem_limit_bytes=48 * 1024 * 1024

time: 24.5 us -> 24.2 us (0.988)
  no operation moved by 1% of the time
where the time goes in v8:
time: 24.2 us; the launch traced here: 24 us
  Pallas kernels  23 us (95%)
  local copies, waits for them, and re-layouts  0.95 us (4%)
    pallas_call x1, Pallas kernels, shards(): pl.pallas_call(functools.partial(kernel, cfg), out_shape=jax.ShapeDtypeSt...  23 us
    unnamed x1, local copies, waits for them, and re-layouts  0.95 us

profile of v8, /device:TPU:1, one launch (start us, length us, event | category | flops | bytes accessed | tf_op | source)
XLA Modules:
  0.0 24.0 jit_solution(10498033826936893984)
XLA Ops:
  0.0 23.0 %jet_section.1 = f32[5,2,96,256]{3,2,1,0:T(8,128)S(1)} custom-call(f32[5,2,96,256]{3,2,1,0:T(8,128)} %bitcast.5, f32[5,2,96,256]{3,2,1,0:T(8,128)} %bitcast.6, s32[1,64]{1,0:T(1,128)} %bitcast.7, bf16[720,256]{1,0:T(8,128)(2,1)} %constant.4.clone.table_hbm, bf16[3072,256]{1,0:T(8,128)(2,1)} %constant.5.clone.bases_hbm), custom_call_target="tpu_custom_call" | custom-call | tf_op jit(solution)/shard_map/jet_section/pallas_call | solution.py:547
  23.0 0.9 %copy.7 = f32[5,2,256,96]{2,3,1,0:T(8,128)} copy(f32[5,2,256,96]{2,3,1,0:T(8,128)S(1)} %bitcast.4) | data formatting | bytes 1966080

commit v9 on v8

--- a/solution.py
+++ b/solution.py
@@ -98,11 +98,10 @@
 
 def pieces_of(inner, cycles):
     span = inner // CHUNKS
-    half = span // 2
     packed = PACKED * GROUP
     pieces = [(inner, cycles - inner), (packed, span - packed), (0, packed)]
     pieces += [(c * span, span) for c in range(1, CHUNKS - 1)]
-    return pieces + [(inner - span, half), (inner - half, half // 2), (inner - half // 2, half // 2)]
+    return pieces + [(inner - span, span - TILE), (inner - TILE, TILE)]
 
 
 def split(values):

time: 24.2 us -> 24.1 us (level)
  no operation moved by 1% of the time
where the time goes in v9:
time: 24.1 us; the launch traced here: 23.9 us
  Pallas kernels  23 us (95%)
  local copies, waits for them, and re-layouts  0.95 us (4%)
    pallas_call x1, Pallas kernels, shards(): pl.pallas_call(functools.partial(kernel, cfg), out_shape=jax.ShapeDtypeSt...  23 us
    unnamed x1, local copies, waits for them, and re-layouts  0.95 us

profile of v9, /device:TPU:1, one launch (start us, length us, event | category | flops | bytes accessed | tf_op | source)
XLA Modules:
  0.0 23.9 jit_solution(10998931585150009402)
XLA Ops:
  0.0 23.0 %jet_section.1 = f32[5,2,96,256]{3,2,1,0:T(8,128)S(1)} custom-call(f32[5,2,96,256]{3,2,1,0:T(8,128)} %bitcast.5, f32[5,2,96,256]{3,2,1,0:T(8,128)} %bitcast.6, s32[1,64]{1,0:T(1,128)} %bitcast.7, bf16[720,256]{1,0:T(8,128)(2,1)} %constant.4.clone.table_hbm, bf16[3072,256]{1,0:T(8,128)(2,1)} %constant.5.clone.bases_hbm), custom_call_target="tpu_custom_call" | custom-call | tf_op jit(solution)/shard_map/jet_section/pallas_call | solution.py:546
  23.0 0.9 %copy.7 = f32[5,2,256,96]{2,3,1,0:T(8,128)} copy(f32[5,2,256,96]{2,3,1,0:T(8,128)S(1)} %bitcast.4) | data formatting | bytes 1966080

commit v10 on v9

--- a/solution.py
+++ b/solution.py
@@ -250,8 +250,9 @@
     ]
 
     pl.semaphore_wait(barrier, 2 + level + level_mates)
-    for copy in crossings[0]:
-        copy.start()
+    last_core = lax.rem(a, 2) == 1
+    pl.when(last_core)(crossings[0][0].start)
+    pl.when(jnp.logical_not(last_core))(crossings[0][1].start)
     for device, earlier in zip(azim_peers, is_earlier):
         pl.when(earlier)(functools.partial(greet, device, answered))
 
@@ -307,6 +308,8 @@
             for copy in moments[c]:
                 copy.start()
 
+    pl.when(last_core)(crossings[0][1].start)
+    pl.when(jnp.logical_not(last_core))(crossings[0][0].start)
     local_high, local_low = table[pl.ds(0, width), :], table[pl.ds(width, width), :]
     for c in range(CHUNKS):
         near[c] = mm(x_high[c], local_high) + mm(x_low[c], local_high) + mm(x_high[c], local_low)

time: 24.1 us -> 24.1 us (level)
  no operation moved by 1% of the time
where the time goes in v10:
time: 24.1 us; the launch traced here: 23.9 us
  Pallas kernels  23 us (95%)
  local copies, waits for them, and re-layouts  0.95 us (4%)
    pallas_call x1, Pallas kernels, shards(): pl.pallas_call(functools.partial(kernel, cfg), out_shape=jax.ShapeDtypeSt...  23 us
    unnamed x1, local copies, waits for them, and re-layouts  0.95 us

profile of v10, /device:TPU:1, one launch (start us, length us, event | category | flops | bytes accessed | tf_op | source)
XLA Modules:
  0.0 23.9 jit_solution(1289206135918421526)
XLA Ops:
  0.0 23.0 %jet_section.1 = f32[5,2,96,256]{3,2,1,0:T(8,128)S(1)} custom-call(f32[5,2,96,256]{3,2,1,0:T(8,128)} %bitcast.5, f32[5,2,96,256]{3,2,1,0:T(8,128)} %bitcast.6, s32[1,64]{1,0:T(1,128)} %bitcast.7, bf16[720,256]{1,0:T(8,128)(2,1)} %constant.4.clone.table_hbm, bf16[3072,256]{1,0:T(8,128)(2,1)} %constant.5.clone.bases_hbm), custom_call_target="tpu_custom_call" | custom-call | tf_op jit(solution)/shard_map/jet_section/pallas_call | solution.py:549
  23.0 0.9 %copy.7 = f32[5,2,256,96]{2,3,1,0:T(8,128)} copy(f32[5,2,256,96]{2,3,1,0:T(8,128)S(1)} %bitcast.4) | data formatting | bytes 1966080

commit v11 on v9

--- a/solution.py
+++ b/solution.py
@@ -101,7 +101,7 @@
     packed = PACKED * GROUP
     pieces = [(inner, cycles - inner), (packed, span - packed), (0, packed)]
     pieces += [(c * span, span) for c in range(1, CHUNKS - 1)]
-    return pieces + [(inner - span, span - TILE), (inner - TILE, TILE)]
+    return pieces + [(inner - span, span - 2 * TILE), (inner - 2 * TILE, 2 * TILE)]
 
 
 def split(values):
@@ -360,8 +360,9 @@
                 axial_flux(values, x, rows)
             for end, pair in ends:
                 if 0 < end - (c * span + first) <= BLOCK:
-                    for copy in pair:
-                        copy.start()
+                    pair[1].start()
+                    if end < inner:
+                        pair[0].start()
         if c == 0:
             loads[4].wait()
             tiles = [
@@ -472,6 +473,8 @@
             jnp.where(ghost_row == 1, pltpu.roll(tile, 1, 0), 0.0),
         )
         rate[f, x, pl.ds(0, 8), :] = rate[f, x, pl.ds(0, 8), :] + ghost_scale * inside
+
+    crossings[-1][0].start()
 
     def raw_flux(ref, x, rows):
         values = [ref[f, x, rows, :] for f in range(fields)]

time: 24.1 us -> 24.2 us (level)
  the two profiles are of different devices: /device:TPU:1 before, /device:TPU:0 now
where the time goes in v11:
time: 24.2 us; the launch traced here: 24.1 us
  Pallas kernels  23.1 us (95%)
  local copies, waits for them, and re-layouts  0.95 us (4%)
    pallas_call x1, Pallas kernels, shards(): pl.pallas_call(functools.partial(kernel, cfg), out_shape=jax.ShapeDtypeSt...  23.1 us
    unnamed x1, local copies, waits for them, and re-layouts  0.95 us

profile of v11, /device:TPU:0, one launch (start us, length us, event | category | flops | bytes accessed | tf_op | source)
XLA Modules:
  0.0 24.1 jit_solution(17539477198747047922)
XLA Ops:
  0.0 23.1 %jet_section.1 = f32[5,2,96,256]{3,2,1,0:T(8,128)S(1)} custom-call(f32[5,2,96,256]{3,2,1,0:T(8,128)} %bitcast.5, f32[5,2,96,256]{3,2,1,0:T(8,128)} %bitcast.6, s32[1,64]{1,0:T(1,128)} %bitcast.7, bf16[720,256]{1,0:T(8,128)(2,1)} %constant.4.clone.table_hbm, bf16[3072,256]{1,0:T(8,128)(2,1)} %constant.5.clone.bases_hbm), custom_call_target="tpu_custom_call" | custom-call | tf_op jit(solution)/shard_map/jet_section/pallas_call | solution.py:549
  23.1 0.9 %copy.7 = f32[5,2,256,96]{2,3,1,0:T(8,128)} copy(f32[5,2,256,96]{2,3,1,0:T(8,128)S(1)} %bitcast.4) | data formatting | bytes 1966080
